TPU v7x, 32 devices: a whole 2x2x4 slice. The times are simulated.
32 devices in a mesh: dp: 4 (over y, x), sp: 8 (over z, core).
Axes of the slice: x: 2, y: 2, z: 4, core: 2. Of those that a mesh axis runs over, the one named last changes fastest.
Arguments:
- first_layer_input: bfloat16 [8, 1024, 1024], P('dp', 'sp'), may hold values from -6 to 6
- cotangent: bfloat16 [8, 1024, 1024], P('dp', 'sp'), may hold values from -6 to 6
- document_begin: int32 [8, 1024], P('dp'), may hold values from 0 to 1023, as said below
- query_key_value_weight: bfloat16 [2, 1024, 3072], P(None, 'dp'), may hold values from -0.1875 to 0.1875
- attention_out_weight: bfloat16 [2, 1024, 1024], P(None, 'dp'), may hold values from -0.5 to 0.5
- feedforward_in_weight: bfloat16 [2, 1024, 4096], P(None, 'dp'), may hold values from -0.1875 to 0.1875
- feedforward_out_weight: bfloat16 [2, 4096, 1024], P(None, 'dp'), may hold values from -0.09375 to 0.09375
- query_value_bias: float32 [2, 2, 1024], replicated, may hold values from -3 to 3
- attention_out_bias: float32 [2, 1024], replicated, may hold values from -2 to 2
- feedforward_in_bias: float32 [2, 4096], replicated, may hold values from -2 to 2
- feedforward_out_bias: float32 [2, 1024], replicated, may hold values from -2 to 2
- layernorm_gain: float32 [2, 2, 1024], replicated, may hold values from 0.25 to 1.75
- layernorm_bias: float32 [2, 2, 1024], replicated, may hold values from -2 to 2
- adapter_down_maps: float32 [2, 2, 4, 1024], replicated, may hold values from -0.1875 to 0.1875
- adapter_up_maps: float32 [2, 2, 4, 1024], replicated, may hold values from -0.3 to 0.3
Outputs:
- output: float32 [8, 1024, 1024], P('dp', 'sp')
- input_grad: float32 [8, 1024, 1024], P('dp', 'sp')
- grad_down: float32 [2, 2, 4, 1024], replicated
- grad_up: float32 [2, 2, 4, 1024], replicated
Inputs may be any that keep to these rules, and one draw needn't show every extreme that they name: document_begin[s, t] is the first position of the document that holds token t of slot s: 0 at t = 0, never falling along a slot, equal to t where a document begins and constant inside a document. Of every aligned group of 2 slots, one is a single document; in every other slot the last token is a document of its own.
All inputs are finite; a program needn't handle non-finite values.
Results may differ from a plain program's by a relative error of at most 0.014.
Values may be sent and summed in bfloat16 or wider, within the bound.
A program may use at most 192 MiB of HBM per device.

v0:
```python
from functools import partial
import math

import jax
import jax.numpy as jnp
from jax import lax
from jax.sharding import PartitionSpec as P

HEAD_SIZE = 64


EPSILON = 1e-05
ADAPTER_ALPHA = 32.0
EXACT_PRECISION = lax.Precision.HIGHEST
MASKED = -1e30


def layer_norm(tensor, gains, shifts):
    row_mean = jnp.mean(tensor, -1, keepdims=True)
    centred = tensor - row_mean
    spread = jnp.mean(centred * centred, -1, keepdims=True)
    return centred * lax.rsqrt(spread + EPSILON) * gains + shifts


def fetch_weights(
    query_key_value_weight,
    attention_out_weight,
    feedforward_in_weight,
    feedforward_out_weight,
    layer_number,
):
    return (
        lax.all_gather(query_key_value_weight[layer_number], "dp", axis=0, tiled=True),
        lax.all_gather(attention_out_weight[layer_number], "dp", axis=0, tiled=True),
        lax.all_gather(feedforward_in_weight[layer_number], "dp", axis=0, tiled=True),
        lax.all_gather(feedforward_out_weight[layer_number], "dp", axis=0, tiled=True),
    )


def sum_adapters(down_terms, up_terms):
    return lax.psum((down_terms, up_terms), ("dp", "sp"))


def slot_scores(query_rows, key_rows, document_starts):
    length = query_rows.shape[0]
    heads_q = query_rows.reshape(length, -1, HEAD_SIZE)
    heads_k = key_rows.reshape(length, -1, HEAD_SIZE)
    scores = jnp.einsum("qhd,khd->hqk", heads_q, heads_k, preferred_element_type=jnp.float32)
    places = jnp.arange(length)
    allowed = (document_starts[:, None] == document_starts[None, :]) & (
        places[None, :] <= places[:, None]
    )
    return jnp.where(allowed[None], scores, MASKED)


def slot_forward(slot_items):
    query_rows, key_rows, value_rows, document_starts = slot_items
    length = query_rows.shape[0]
    scores = slot_scores(query_rows, key_rows, document_starts)
    row_max = jnp.max(scores, -1, keepdims=True)
    row_total = jnp.sum(jnp.exp(scores - row_max), -1, keepdims=True)
    log_total = row_max + jnp.log(row_total)
    probability = jnp.exp(scores - log_total).astype(jnp.bfloat16)
    mixture = jnp.einsum(
        "hqk,khd->qhd",
        probability,
        value_rows.reshape(length, -1, HEAD_SIZE),
        preferred_element_type=jnp.float32,
    )
    return (mixture.reshape(length, -1).astype(jnp.bfloat16), log_total[..., 0])


def slot_backward(slot_items):
    query_rows, key_rows, value_rows, document_starts, log_total, grad_mixture = slot_items
    length = query_rows.shape[0]
    scores = slot_scores(query_rows, key_rows, document_starts)
    probability = jnp.exp(scores - log_total[..., None])
    low_probability = probability.astype(jnp.bfloat16)
    grad_heads = grad_mixture.reshape(length, -1, HEAD_SIZE)
    value_heads = value_rows.reshape(length, -1, HEAD_SIZE)
    grad_values = jnp.einsum(
        "hqk,qhd->khd", low_probability, grad_heads, preferred_element_type=jnp.float32
    )
    grad_prob = jnp.einsum(
        "qhd,khd->hqk", grad_heads, value_heads, preferred_element_type=jnp.float32
    )
    grad_scores = probability * (grad_prob - jnp.sum(probability * grad_prob, -1, keepdims=True))
    low_scores = grad_scores.astype(jnp.bfloat16)
    grad_queries = jnp.einsum(
        "hqk,khd->qhd",
        low_scores,
        key_rows.reshape(length, -1, HEAD_SIZE),
        preferred_element_type=jnp.float32,
    )
    grad_keys = jnp.einsum(
        "hqk,qhd->khd",
        low_scores,
        query_rows.reshape(length, -1, HEAD_SIZE),
        preferred_element_type=jnp.float32,
    )
    return (
        grad_queries.reshape(length, -1).astype(jnp.bfloat16),
        grad_keys.reshape(length, -1).astype(jnp.bfloat16),
        grad_values.reshape(length, -1).astype(jnp.bfloat16),
    )


def layer_forward(hidden_state, weight_set, params, document_begin):
    query_key_value_weight, attention_out_weight, feedforward_in_weight, feedforward_out_weight = (
        weight_set
    )
    (
        query_value_bias,
        attention_out_bias,
        feedforward_in_bias,
        feedforward_out_bias,
        gains,
        shifts,
        down_projection,
        up_projection,
    ) = params
    model_dimension = hidden_state.shape[-1]
    normed = layer_norm(hidden_state, gains[0], shifts[0]).astype(jnp.bfloat16)
    projected_rows = jnp.einsum(
        "std,de->ste", normed, query_key_value_weight, preferred_element_type=jnp.float32
    )
    widened = normed.astype(jnp.float32)
    adapter_scale = ADAPTER_ALPHA / down_projection.shape[1]
    query_row_block = jnp.einsum(
        "nyh,lh->nyl", widened, down_projection[0], precision=EXACT_PRECISION
    )
    value_row_block = jnp.einsum(
        "nyh,lh->nyl", widened, down_projection[1], precision=EXACT_PRECISION
    )
    query_rows = (
        (
            projected_rows[..., :model_dimension]
            + query_value_bias[0]
            + adapter_scale
            * jnp.einsum(
                "wah,hp->wap", query_row_block, up_projection[0], precision=EXACT_PRECISION
            )
        )
        * HEAD_SIZE ** (-0.5)
    ).astype(jnp.bfloat16)
    key_rows = projected_rows[..., model_dimension : 2 * model_dimension].astype(jnp.bfloat16)
    value_rows = (
        projected_rows[..., 2 * model_dimension :]
        + query_value_bias[1]
        + adapter_scale
        * jnp.einsum("wah,hp->wap", value_row_block, up_projection[1], precision=EXACT_PRECISION)
    ).astype(jnp.bfloat16)
    queries_h, keys_h, values_h = (
        lax.all_to_all(query_rows, "sp", split_axis=2, concat_axis=1, tiled=True),
        lax.all_to_all(key_rows, "sp", split_axis=2, concat_axis=1, tiled=True),
        lax.all_to_all(value_rows, "sp", split_axis=2, concat_axis=1, tiled=True),
    )
    mixture_h, log_total = lax.map(slot_forward, (queries_h, keys_h, values_h, document_begin))
    mixture = lax.all_to_all(mixture_h, "sp", split_axis=1, concat_axis=2, tiled=True)
    attended = hidden_state + (
        jnp.einsum("std,de->ste", mixture, attention_out_weight, preferred_element_type=jnp.float32)
        + attention_out_bias
    )
    normed_mlp = layer_norm(attended, gains[1], shifts[1]).astype(jnp.bfloat16)
    pre_act = (
        jnp.einsum(
            "std,df->stf", normed_mlp, feedforward_in_weight, preferred_element_type=jnp.float32
        )
        + feedforward_in_bias
    )
    activation = jax.nn.gelu(pre_act, approximate=True).astype(jnp.bfloat16)
    final_result = attended + (
        jnp.einsum(
            "stf,fd->std", activation, feedforward_out_weight, preferred_element_type=jnp.float32
        )
        + feedforward_out_bias
    )
    saved_state = (
        normed,
        query_row_block,
        value_row_block,
        queries_h,
        keys_h,
        values_h,
        log_total,
        attended,
        pre_act,
    )
    return (final_result, saved_state)


def layer_backward(hidden_state, gradient, weight_set, params, document_begin, saved_state):
    query_key_value_weight, attention_out_weight, feedforward_in_weight, feedforward_out_weight = (
        weight_set
    )
    (
        query_value_bias,
        attention_out_bias,
        feedforward_in_bias,
        feedforward_out_bias,
        gains,
        shifts,
        down_projection,
        up_projection,
    ) = params
    (
        normed,
        query_row_block,
        value_row_block,
        queries_h,
        keys_h,
        values_h,
        log_total,
        attended,
        pre_act,
    ) = saved_state
    grad_act = jnp.einsum(
        "std,fd->stf",
        gradient.astype(jnp.bfloat16),
        feedforward_out_weight,
        preferred_element_type=jnp.float32,
    )
    unused_act, gelu_back = jax.vjp(partial(jax.nn.gelu, approximate=True), pre_act)
    grad_pre = gelu_back(grad_act)[0].astype(jnp.bfloat16)
    grad_normed_mlp = jnp.einsum(
        "stf,df->std", grad_pre, feedforward_in_weight, preferred_element_type=jnp.float32
    )
    unused_norm, second_back = jax.vjp(
        lambda tensor: layer_norm(tensor, gains[1], shifts[1]), attended
    )
    grad_attended = gradient + second_back(grad_normed_mlp)[0]
    grad_mixture = jnp.einsum(
        "ste,de->std",
        grad_attended.astype(jnp.bfloat16),
        attention_out_weight,
        preferred_element_type=jnp.float32,
    ).astype(jnp.bfloat16)
    grad_mixture_h = lax.all_to_all(grad_mixture, "sp", split_axis=2, concat_axis=1, tiled=True)
    grad_q_h, grad_k_h, grad_v_h = lax.map(
        slot_backward, (queries_h, keys_h, values_h, document_begin, log_total, grad_mixture_h)
    )
    grad_queries, grad_keys, grad_values = (
        lax.all_to_all(grad_q_h, "sp", split_axis=1, concat_axis=2, tiled=True),
        lax.all_to_all(grad_k_h, "sp", split_axis=1, concat_axis=2, tiled=True),
        lax.all_to_all(grad_v_h, "sp", split_axis=1, concat_axis=2, tiled=True),
    )
    grad_queries = grad_queries * jnp.asarray(HEAD_SIZE ** (-0.5), jnp.bfloat16)
    stacked = jnp.concatenate([grad_queries, grad_keys, grad_values], -1)
    grad_normed = jnp.einsum(
        "ste,de->std", stacked, query_key_value_weight, preferred_element_type=jnp.float32
    )
    adapter_scale = ADAPTER_ALPHA / down_projection.shape[1]
    widened = normed.astype(jnp.float32)
    query_widened = grad_queries.astype(jnp.float32)
    value_widened = grad_values.astype(jnp.float32)
    query_row_gradient = adapter_scale * jnp.einsum(
        "nyh,lh->nyl", query_widened, up_projection[0], precision=EXACT_PRECISION
    )
    value_row_gradient = adapter_scale * jnp.einsum(
        "nyh,lh->nyl", value_widened, up_projection[1], precision=EXACT_PRECISION
    )
    query_up_weight = adapter_scale * jnp.einsum(
        "fkp,fkz->pz", query_row_block, query_widened, precision=EXACT_PRECISION
    )
    value_up_weight = adapter_scale * jnp.einsum(
        "fkp,fkz->pz", value_row_block, value_widened, precision=EXACT_PRECISION
    )
    down_q = jnp.einsum("fkp,fkz->pz", query_row_gradient, widened, precision=EXACT_PRECISION)
    down_v = jnp.einsum("fkp,fkz->pz", value_row_gradient, widened, precision=EXACT_PRECISION)
    grad_normed = (
        grad_normed
        + jnp.einsum(
            "wah,hp->wap", query_row_gradient, down_projection[0], precision=EXACT_PRECISION
        )
        + jnp.einsum(
            "wah,hp->wap", value_row_gradient, down_projection[1], precision=EXACT_PRECISION
        )
    )
    unused_first, first_back = jax.vjp(
        lambda tensor: layer_norm(tensor, gains[0], shifts[0]), hidden_state
    )
    grad_hidden = grad_attended + first_back(grad_normed)[0]
    return (grad_hidden, jnp.stack([down_q, down_v]), jnp.stack([query_up_weight, value_up_weight]))


def body(
    first_layer_input,
    cotangent,
    document_begin,
    query_key_value_weight,
    attention_out_weight,
    feedforward_in_weight,
    feedforward_out_weight,
    query_value_bias,
    attention_out_bias,
    feedforward_in_bias,
    feedforward_out_bias,
    layernorm_gain,
    layernorm_bias,
    adapter_down_maps,
    adapter_up_maps,
):
    layers = query_key_value_weight.shape[0]

    def params_of(layer_number):
        return (
            query_value_bias[layer_number],
            attention_out_bias[layer_number],
            feedforward_in_bias[layer_number],
            feedforward_out_bias[layer_number],
            layernorm_gain[layer_number],
            layernorm_bias[layer_number],
            adapter_down_maps[layer_number],
            adapter_up_maps[layer_number],
        )

    hidden_state = first_layer_input.astype(jnp.float32)
    inputs = []
    gathered = []
    for layer_number in range(layers):
        weight_set = fetch_weights(
            query_key_value_weight,
            attention_out_weight,
            feedforward_in_weight,
            feedforward_out_weight,
            layer_number,
        )
        inputs.append(hidden_state)
        gathered.append(weight_set)
        hidden_state, unused_state = layer_forward(
            hidden_state, weight_set, params_of(layer_number), document_begin
        )
    gradient = cotangent.astype(jnp.float32)
    down_parts = [None] * layers
    up_parts = [None] * layers
    for layer_number in reversed(range(layers)):
        weight_set = fetch_weights(
            query_key_value_weight,
            attention_out_weight,
            feedforward_in_weight,
            feedforward_out_weight,
            layer_number,
        )
        unused_result, saved_state = layer_forward(
            inputs[layer_number], weight_set, params_of(layer_number), document_begin
        )
        gradient, down_terms, up_terms = layer_backward(
            inputs[layer_number],
            gradient,
            weight_set,
            params_of(layer_number),
            document_begin,
            saved_state,
        )
        down_parts[layer_number] = down_terms
        up_parts[layer_number] = up_terms
    grad_down = jnp.stack(down_parts)
    grad_up = jnp.stack(up_parts)
    grad_down, grad_up = sum_adapters(grad_down, grad_up)
    tokens = (
        first_layer_input.shape[0]
        * first_layer_input.shape[1]
        * lax.axis_size("dp")
        * lax.axis_size("sp")
    )
    token_scale = 1.0 / math.sqrt(tokens)
    return (hidden_state, gradient, grad_down * token_scale, grad_up * token_scale)


def solution(mesh):
    placed = (
        P("dp", "sp", None),
        P("dp", "sp", None),
        P("dp", None),
        P(None, "dp", None),
        P(None, "dp", None),
        P(None, "dp", None),
        P(None, "dp", None),
        P(),
        P(),
        P(),
        P(),
        P(),
        P(),
        P(),
        P(),
    )
    return jax.shard_map(
        body,
        mesh=mesh,
        in_specs=placed,
        out_specs=(P("dp", "sp", None), P("dp", "sp", None), P(), P()),
        check_vma=False,
    )
```

profile of v0, /device:TPU:0, one launch (start us, length us, event | category | flops | bytes accessed | tf_op | source)
XLA Modules:
  0.0 1025.3 jit_solution(3215920100778661397)
XLA Ops:
  25.0 59.0 %all-gather.17.cloned.1.call-done = bf16[1,1024,3072]{2,1,0:T(8,128)(2,1)} async-done(((bf16[1,256,3072]{2,1,0:T(8,128)(2,1)}), bf16[1,1024,3072]{2,1,0:T(8,128)(2,1)}) %all-gather.17.cloned.1.call-update) | async-done | bytes 6291472 | tf_op jit(solution)/shard_map/all_gather | solution.py:33
  101.4 11.2 %all-to-all-done = bf16[2,128,1024]{1,0,2:T(2,128)(2,1)S(1)} async-done(((bf16[2,128,1024]{1,0,2:T(2,128)(2,1)}), bf16[2,128,1024]{1,0,2:T(2,128)(2,1)S(1)}, u32[]{:S(2)}, u32[]{:S(2)}) %all-to-all-start) | async-done | bytes 524320 | tf_op jit(solution)/shard_map/all_to_all | solution.py:156
  118.6 12.9 %all-to-all-done.1 = bf16[2,128,1024]{1,0,2:T(2,128)(2,1)S(1)} async-done(((bf16[2,128,1024]{1,0,2:T(2,128)(2,1)}), bf16[2,128,1024]{1,0,2:T(2,128)(2,1)S(1)}, u32[]{:S(2)}, u32[]{:S(2)}) %all-to-all-start.1) | async-done | bytes 524320 | tf_op jit(solution)/shard_map/all_to_all | solution.py:154
  136.9 13.3 %all-to-all-done.2 = bf16[2,128,1024]{1,0,2:T(2,128)(2,1)S(1)} async-done(((bf16[2,128,1024]{1,0,2:T(2,128)(2,1)}), bf16[2,128,1024]{1,0,2:T(2,128)(2,1)S(1)}, u32[]{:S(2)}, u32[]{:S(2)}) %all-to-all-start.2) | async-done | bytes 524320 | tf_op jit(solution)/shard_map/all_to_all | solution.py:155
  150.9 12.9 %while.72 = (s32[]{:T(128)}, bf16[2,1024,128]{1,2,0:T(8,128)(2,1)S(1)}, bf16[2,1024,128]{1,2,0:T(8,128)(2,1)S(1)}, s32[2,1024]{1,0:T(2,128)S(1)}, bf16[2,1024,12...) while((s32[]{:T(128)}, bf16[2,1024,128]{1,2,0:T(8,128)(2,1)S(1)}, ...), condition=%wide.region_5.6_spmd, body=%wide.region_2.5_spmd.sunk | while | flops 556922880 | bytes 32575588 | solution.py:158
  169.3 14.6 %all-to-all-done.3 = bf16[2,1024,128]{2,0,1:T(2,128)(2,1)S(1)} async-done(((bf16[2,1024,128]{2,0,1:T(2,128)(2,1)}), bf16[2,1024,128]{2,0,1:T(2,128)(2,1)S(1)}, u32[]{:S(2)}, u32[]{:S(2)}) %all-to-all-start.3) | async-done | bytes 524320 | tf_op jit(solution)/shard_map/all_to_all | solution.py:159
  188.2 22.6 %all-gather.23.cloned.1.call-done = bf16[1,4096,1024]{2,1,0:T(8,128)(2,1)} async-done(((bf16[1,1024,1024]{2,1,0:T(8,128)(2,1)}), bf16[1,4096,1024]{2,1,0:T(8,128)(2,1)}) %all-gather.23.cloned.1.call-update) | async-done | bytes 8388624 | tf_op jit(solution)/shard_map/all_gather | solution.py:36
  210.8 89.3 %all-gather.21.cloned.1.call-done = bf16[1,1024,4096]{2,1,0:T(8,128)(2,1)} async-done(((bf16[1,256,4096]{2,1,0:T(8,128)(2,1)}), bf16[1,1024,4096]{2,1,0:T(8,128)(2,1)}) %all-gather.21.cloned.1.call-update) | async-done | bytes 8388624 | tf_op jit(solution)/shard_map/all_gather | solution.py:35
  300.1 11.5 %fusion.337 = (f32[2,128]{1,0:T(2,128)S(1)}, f32[2,128,1024]{2,1,0:T(8,128)S(1)}) fusion(f32[2,128,1024]{2,1,0:T(8,128)} %copy-done.51, f32[1024]{0:T(1024)S(1)} %bitcast.735, bf16[1,4096,1024]{2,1,0:T(8,128)(2,1)} %all-gather.23.cloned.1.call-done, bf16[1,1024,4096]{2,1,0:T(8,128)(2,1)} %all-gather.21.cloned.1.call-done, f32[4096]{0:T(1024)S(1)} %bitcast.730, ...), kind=kOutput, calls=%fused_computation.425 | convolution fusion | flops 4307550208 | bytes 18906112 | tf_op jit(solution)/shard_map/stf,fd->std/dot_general | solution.py:173
  313.4 58.7 %all-gather.25.cloned.1.call-done = bf16[1,1024,3072]{2,1,0:T(8,128)(2,1)} async-done(((bf16[1,256,3072]{2,1,0:T(8,128)(2,1)}), bf16[1,1024,3072]{2,1,0:T(8,128)(2,1)}) %all-gather.25.cloned.1.call-update) | async-done | bytes 6291472 | tf_op jit(solution)/shard_map/all_gather | solution.py:33
  409.8 11.2 %all-to-all-done.5 = bf16[2,128,1024]{1,0,2:T(2,128)(2,1)S(1)} async-done(((bf16[2,128,1024]{1,0,2:T(2,128)(2,1)}), bf16[2,128,1024]{1,0,2:T(2,128)(2,1)S(1)}, u32[]{:S(2)}, u32[]{:S(2)}) %all-to-all-start.5) | async-done | bytes 524320 | tf_op jit(solution)/shard_map/all_to_all | solution.py:154
  446.1 16.5 %while.74 = (s32[]{:T(128)}, bf16[2,1024,128]{1,2,0:T(8,128)(2,1)}, f32[2,2,1024]{2,1,0:T(2,128)S(1)}, bf16[2,1024,128]{1,2,0:T(8,128)(2,1)S(1)}, s32[2,1024]{1,...) while((s32[]{:T(128)}, bf16[2,1024,128]{1,2,0:T(8,128)(2,1)}, ...), condition=%wide.region_19.20_spmd, body=%wide.region_16.19_spmd.sunk | while | flops 556922880 | bytes 36778152 | solution.py:158
  468.9 15.4 %all-to-all-done.8 = bf16[2,1024,128]{2,0,1:T(2,128)(2,1)} async-done(((bf16[2,1024,128]{2,0,1:T(2,128)(2,1)}), bf16[2,1024,128]{2,0,1:T(2,128)(2,1)}, u32[]{:S(2)}, u32[]{:S(2)}) %all-to-all-start.8) | async-done | bytes 524320 | tf_op jit(solution)/shard_map/all_to_all | solution.py:159
  507.1 81.4 %all-gather.31.cloned.1.call-done = bf16[1,4096,1024]{2,1,0:T(8,128)(2,1)} async-done(((bf16[1,1024,1024]{2,1,0:T(8,128)(2,1)}), bf16[1,4096,1024]{2,1,0:T(8,128)(2,1)}) %all-gather.31.cloned.1.call-update) | async-done | bytes 8388624 | tf_op jit(solution)/shard_map/all_gather | solution.py:36
  588.5 12.2 %multiply_reduce_fusion.5 = (f32[2,128]{1,0:T(2,128)S(1)}, f32[2,128,1024]{2,1,0:T(8,128)}) fusion(f32[2,128,1024]{2,1,0:T(8,128)S(1)} %copy-done.22, f32[2,128]{1,0:T(2,128)S(1)} %broadcast_multiply_fusion.5, f32[1024]{0:T(1024)S(1)} %bitcast.744, bf16[1,1024,4096]{2,1,0:T(8,128)(2,1)} %all-gather.29.cloned.1.call-done, f32[2,128,4096]{2,1,0:T(8,128)} %fusion.75, ...), kind=kOutput, calls=%fused_computation.279 | convolution fusion | flops 4316987392 | bytes 23599104 | tf_op jit(solution)/shard_map/stf,df->std/dot_general | solution.py:225
  613.3 15.4 %while.76 = (s32[]{:T(128)}, bf16[2,1024,128]{1,2,0:T(8,128)(2,1)}, f32[2,2,1024]{2,1,0:T(2,128)}, bf16[2,1024,128]{1,2,0:T(8,128)(2,1)S(1)}, s32[2,1024]{1,0:T(...) while((s32[]{:T(128)}, bf16[2,1024,128]{1,2,0:T(8,128)(2,1)}, ...), condition=%wide.region_32.33_spmd, body=%wide.region_29.32_spmd.sunk | while | flops 556922880 | bytes 32583792 | solution.py:158
  643.3 27.2 %while.75 = (s32[]{:T(128)}, bf16[2,1024,128]{1,2,0:T(8,128)(2,1)}, bf16[2,1024,128]{1,2,0:T(8,128)(2,1)}, bf16[2,1024,128]{1,2,0:T(8,128)(2,1)}, bf16[2,1024,12...) while((s32[]{:T(128)}, bf16[2,1024,128]{1,2,0:T(8,128)(2,1)}, ...), condition=%wide.region_26.27_spmd, body=%wide.region_24.26_spmd.sunk | while | flops 1370880000 | bytes 88150360 | solution.py:239
  716.0 12.9 %while.73 = (s32[]{:T(128)}, bf16[2,1024,128]{1,2,0:T(8,128)(2,1)S(1)}, bf16[2,1024,128]{1,2,0:T(8,128)(2,1)S(1)}, s32[2,1024]{1,0:T(2,128)S(1)}, bf16[2,1024,12...) while((s32[]{:T(128)}, bf16[2,1024,128]{1,2,0:T(8,128)(2,1)S(1)}, ...), condition=%wide.region_13.14_spmd, body=%wide.region_10.13_spmd.sunk | while | flops 556922880 | bytes 32575588 | solution.py:158
  749.0 11.9 %multiply_reduce_fusion.2 = (f32[2,128]{1,0:T(2,128)S(1)}, f32[2,128,1024]{2,1,0:T(8,128)}) fusion(f32[2,128,1024]{2,1,0:T(8,128)S(1)} %copy-done.29, f32[2,128]{1,0:T(2,128)S(1)} %broadcast_multiply_fusion.4, f32[1024]{0:T(1024)S(1)} %bitcast.748, bf16[1,1024,4096]{2,1,0:T(8,128)(2,1)} %all-gather.21.cloned.1.call-done, f32[2,128,4096]{2,1,0:T(8,128)} %fusion.69, ...), kind=kOutput, calls=%fused_computation.273 | convolution fusion | flops 4317249536 | bytes 24123392 | tf_op jit(solution)/shard_map/stf,df->std/dot_general | solution.py:225
  792.7 28.4 %while.77 = (s32[]{:T(128)}, bf16[2,1024,128]{1,2,0:T(8,128)(2,1)}, bf16[2,1024,128]{1,2,0:T(8,128)(2,1)}, bf16[2,1024,128]{1,2,0:T(8,128)(2,1)}, bf16[2,1024,12...) while((s32[]{:T(128)}, bf16[2,1024,128]{1,2,0:T(8,128)(2,1)}, ...), condition=%wide.region_39.40_spmd, body=%wide.region_37.39_spmd.sunk | while | flops 1370880000 | bytes 86053176 | solution.py:239
  830.7 11.2 %all-to-all-done.17 = bf16[2,1024,128]{2,0,1:T(2,128)(2,1)S(1)} async-done(((bf16[2,1024,128]{2,0,1:T(2,128)(2,1)}), bf16[2,1024,128]{2,0,1:T(2,128)(2,1)S(1)}, u32[]{:S(2)}, u32[]{:S(2)}) %all-to-all-start.17) | async-done | bytes 524320 | tf_op jit(solution)/shard_map/all_to_all | solution.py:245
  846.5 12.0 %fusion.191 = f32[2,128,1024]{2,1,0:T(8,128)} fusion(f32[2,128,1024]{2,1,0:T(8,128)S(1)} %get-tuple-element.421, bf16[1,4096,1024]{2,1,0:T(8,128)(2,1)} %all-gather.31.cloned.1.call-done, bf16[1,1024,4096]{2,1,0:T(8,128)(2,1)} %all-gather.29.cloned.1.call-done, f32[4096]{0:T(1024)S(1)} %bitcast.729, f32[1024]{0:T(1024)S(1)} %bitcast.732, ...), kind=kOutput, calls=%fused_computation.233 | convolution fusion | flops 4307288064 | bytes 18905088 | tf_op jit(solution)/shard_map/stf,fd->std/dot_general | solution.py:173
  871.8 11.3 %all-to-all-done.16 = bf16[2,1024,128]{2,0,1:T(2,128)(2,1)S(1)} async-done(((bf16[2,1024,128]{2,0,1:T(2,128)(2,1)}), bf16[2,1024,128]{2,0,1:T(2,128)(2,1)S(1)}, u32[]{:S(2)}, u32[]{:S(2)}) %all-to-all-start.16) | async-done | bytes 524320 | tf_op jit(solution)/shard_map/all_to_all | solution.py:244
  897.1 118.2 %all-reduce.3.cloned.1.call-done = (f32[2,2,4,1024]{3,2,1,0:T(4,128)}, f32[2,2,4,1024]{3,2,1,0:T(4,128)}) async-done(((f32[2,2,4,1024]{3,2,1,0:T(4,128)}, f32[2,2,4,1024]{3,2,1,0:T(4,128)}), (f32[2,2,4,1024]{3,2,1,0:T(4,128)}, f32[2,2,4,1024]{3,2,1,0:T(4,128)})) %all-reduce.3.cloned.1.call-update) | async-done | bytes 131088 | tf_op jit(solution)/shard_map/psum | solution.py:41
  (595 shorter events, 430.2 us)
Async XLA Ops:
  7.2 76.9 %all-gather.17.cloned.1.call-start = ((), (), s32[]{:S(2)}) async-start(), calls=%async_computation.18 | async-start | bytes 7864320 | tf_op jit(solution)/shard_map/all_gather | solution.py:33
  11.0 174.3 %all-gather.19.cloned.1.call-start = ((), (), s32[]{:S(2)}) async-start(), calls=%async_computation.19 | async-start | bytes 2621440 | tf_op jit(solution)/shard_map/all_gather | solution.py:34
  12.1 198.7 %all-gather.23.cloned.1.call-start = ((), (), s32[]{:S(2)}) async-start(), calls=%async_computation.21 | async-start | bytes 10485760 | tf_op jit(solution)/shard_map/all_gather | solution.py:36
  16.8 283.3 %all-gather.21.cloned.1.call-start = ((), (), s32[]{:S(2)}) async-start(), calls=%async_computation.20 | async-start | bytes 10485760 | tf_op jit(solution)/shard_map/all_gather | solution.py:35
  21.8 350.3 %all-gather.25.cloned.1.call-start = ((), (), s32[]{:S(2)}) async-start(), calls=%async_computation.22 | async-start | bytes 7864320 | tf_op jit(solution)/shard_map/all_gather | solution.py:33
  22.4 466.1 %all-gather.27.cloned.1.call-start = ((), (), s32[]{:S(2)}) async-start(), calls=%async_computation.23 | async-start | bytes 2621440 | tf_op jit(solution)/shard_map/all_gather | solution.py:34
  22.9 476.0 %all-gather.29.cloned.1.call-start = ((), (), s32[]{:S(2)}) async-start(), calls=%async_computation.24 | async-start | bytes 10485760 | tf_op jit(solution)/shard_map/all_gather | solution.py:35
  92.7 20.0 %all-to-all-start = ((bf16[2,128,1024]{1,0,2:T(2,128)(2,1)}), bf16[2,128,1024]{1,0,2:T(2,128)(2,1)S(1)}, u32[]{:S(2)}, u32[]{:S(2)}) async-start(bf16[2,128,1024]{1,0,2:T(2,128)(2,1)} %copy.57), calls=%async_computation | async-start | bytes 1048576 | tf_op jit(solution)/shard_map/all_to_all | solution.py:156
  131.4 18.8 %all-to-all-start.2 = ((bf16[2,128,1024]{1,0,2:T(2,128)(2,1)}), bf16[2,128,1024]{1,0,2:T(2,128)(2,1)S(1)}, u32[]{:S(2)}, u32[]{:S(2)}) async-start(bf16[2,128,1024]{1,0,2:T(2,128)(2,1)} %copy.61), calls=%async_computation.2 | async-start | bytes 1048576 | tf_op jit(solution)/shard_map/all_to_all | solution.py:155
  135.0 453.5 %all-gather.31.cloned.1.call-start = ((), (), s32[]{:S(2)}) async-start(), calls=%async_computation.25 | async-start | bytes 10485760 | tf_op jit(solution)/shard_map/all_gather | solution.py:36
  164.9 19.0 %all-to-all-start.3 = ((bf16[2,1024,128]{2,0,1:T(2,128)(2,1)}), bf16[2,1024,128]{2,0,1:T(2,128)(2,1)S(1)}, u32[]{:S(2)}, u32[]{:S(2)}) async-start(bf16[2,1024,128]{2,0,1:T(2,128)(2,1)} %copy.63), calls=%async_computation.3 | async-start | bytes 1048576 | tf_op jit(solution)/shard_map/all_to_all | solution.py:159
  382.1 20.1 %all-to-all-start.4 = ((bf16[2,128,1024]{1,0,2:T(2,128)(2,1)}), bf16[2,128,1024]{1,0,2:T(2,128)(2,1)}, u32[]{:S(2)}, u32[]{:S(2)}) async-start(bf16[2,128,1024]{1,0,2:T(2,128)(2,1)} %copy.65), calls=%async_computation.4 | async-start | bytes 1048576 | tf_op jit(solution)/shard_map/all_to_all | solution.py:156
  421.0 20.0 %all-to-all-start.6 = ((bf16[2,128,1024]{1,0,2:T(2,128)(2,1)}), bf16[2,128,1024]{1,0,2:T(2,128)(2,1)}, u32[]{:S(2)}, u32[]{:S(2)}) async-start(bf16[2,128,1024]{1,0,2:T(2,128)(2,1)} %copy.69), calls=%async_computation.6 | async-start | bytes 1048576 | tf_op jit(solution)/shard_map/all_to_all | solution.py:155
  464.6 19.7 %all-to-all-start.8 = ((bf16[2,1024,128]{2,0,1:T(2,128)(2,1)}), bf16[2,1024,128]{2,0,1:T(2,128)(2,1)}, u32[]{:S(2)}, u32[]{:S(2)}) async-start(bf16[2,1024,128]{2,0,1:T(2,128)(2,1)} %copy.73), calls=%async_computation.8 | async-start | bytes 1048576 | tf_op jit(solution)/shard_map/all_to_all | solution.py:159
  606.9 24.2 %all-to-all-start.9 = ((bf16[2,128,1024]{1,0,2:T(2,128)(2,1)}), bf16[2,128,1024]{1,0,2:T(2,128)(2,1)}, u32[]{:S(2)}, u32[]{:S(2)}) async-start(bf16[2,128,1024]{1,0,2:T(2,128)(2,1)} %copy.75), calls=%async_computation.9 | async-start | bytes 1048576 | tf_op jit(solution)/shard_map/all_to_all | solution.py:238
  631.1 41.5 %all-to-all-start.13 = ((bf16[2,1024,128]{2,0,1:T(2,128)(2,1)}), bf16[2,1024,128]{2,0,1:T(2,128)(2,1)}, u32[]{:S(2)}, u32[]{:S(2)}) async-start(bf16[2,1024,128]{2,0,1:T(2,128)(2,1)} %copy.83), calls=%async_computation.13 | async-start | bytes 1048576 | tf_op jit(solution)/shard_map/all_to_all | solution.py:159
  672.6 20.6 %all-to-all-start.12 = ((bf16[2,1024,128]{2,0,1:T(2,128)(2,1)}), bf16[2,1024,128]{2,0,1:T(2,128)(2,1)}, u32[]{:S(2)}, u32[]{:S(2)}) async-start(bf16[2,1024,128]{2,0,1:T(2,128)(2,1)} %copy.81), calls=%async_computation.12 | async-start | bytes 1048576 | tf_op jit(solution)/shard_map/all_to_all | solution.py:245
  693.2 19.2 %all-to-all-start.11 = ((bf16[2,1024,128]{2,0,1:T(2,128)(2,1)}), bf16[2,1024,128]{2,0,1:T(2,128)(2,1)S(1)}, u32[]{:S(2)}, u32[]{:S(2)}) async-start(bf16[2,1024,128]{2,0,1:T(2,128)(2,1)} %copy.79), calls=%async_computation.11 | async-start | bytes 1048576 | tf_op jit(solution)/shard_map/all_to_all | solution.py:244
  712.4 20.6 %all-to-all-start.10 = ((bf16[2,1024,128]{2,0,1:T(2,128)(2,1)}), bf16[2,1024,128]{2,0,1:T(2,128)(2,1)S(1)}, u32[]{:S(2)}, u32[]{:S(2)}) async-start(bf16[2,1024,128]{2,0,1:T(2,128)(2,1)} %copy.77), calls=%async_computation.10 | async-start | bytes 1048576 | tf_op jit(solution)/shard_map/all_to_all | solution.py:243
  733.0 34.0 %all-to-all-start.7 = ((bf16[2,1024,128]{2,0,1:T(2,128)(2,1)}), bf16[2,1024,128]{2,0,1:T(2,128)(2,1)}, u32[]{:S(2)}, u32[]{:S(2)}) async-start(bf16[2,1024,128]{2,0,1:T(2,128)(2,1)} %copy.71), calls=%async_computation.7 | async-start | bytes 1048576 | tf_op jit(solution)/shard_map/all_to_all | solution.py:159
  767.1 20.7 %all-to-all-start.14 = ((bf16[2,128,1024]{1,0,2:T(2,128)(2,1)}), bf16[2,128,1024]{1,0,2:T(2,128)(2,1)S(1)}, u32[]{:S(2)}, u32[]{:S(2)}) async-start(bf16[2,128,1024]{1,0,2:T(2,128)(2,1)} %copy.85), calls=%async_computation.14 | async-start | bytes 1048576 | tf_op jit(solution)/shard_map/all_to_all | solution.py:238
  842.0 20.5 %all-to-all-start.15 = ((bf16[2,1024,128]{2,0,1:T(2,128)(2,1)}), bf16[2,1024,128]{2,0,1:T(2,128)(2,1)}, u32[]{:S(2)}, u32[]{:S(2)}) async-start(bf16[2,1024,128]{2,0,1:T(2,128)(2,1)} %copy.87), calls=%async_computation.15 | async-start | bytes 1048576 | tf_op jit(solution)/shard_map/all_to_all | solution.py:243
  862.5 20.6 %all-to-all-start.16 = ((bf16[2,1024,128]{2,0,1:T(2,128)(2,1)}), bf16[2,1024,128]{2,0,1:T(2,128)(2,1)S(1)}, u32[]{:S(2)}, u32[]{:S(2)}) async-start(bf16[2,1024,128]{2,0,1:T(2,128)(2,1)} %copy.89), calls=%async_computation.16 | async-start | bytes 1048576 | tf_op jit(solution)/shard_map/all_to_all | solution.py:244
  867.7 147.6 %all-reduce.3.cloned.1.call-start = ((), (), s32[]{:S(2)}) async-start(), calls=%async_computation.26 | async-start | bytes 262144 | tf_op jit(solution)/shard_map/psum | solution.py:41
  (132 other events, 4707.4 us)
Sparse Core Ops, SparseCore 0:
  11.1 72.8 all-gather.16
  85.9 35.3 all-gather.18
  123.2 87.5 all-gather.22
  212.5 87.5 all-gather.20
  301.8 70.1 all-gather.24
  373.7 35.6 all-gather.26
  411.3 87.5 all-gather.28
  500.8 87.6 all-gather.30
  894.6 120.6 all-reduce.2
where the time goes:
time: 1030 us
  waiting for transfers between devices  582 us (57%)
  matrix products  183 us (18%)
  local copies, waits for them, and re-layouts  114 us (11%)
  starting transfers between devices  79.7 us (8%)
  other arithmetic  48.3 us (5%)
  between operations  16 us (2%)
    psum x1, waiting for transfers between devices, sum_adapters(): return lax.psum((down_terms, up_terms), ('dp', 'sp'))  118 us
    all_gather x2, waiting for transfers between devices, fetch_weights(): lax.all_gather(query_key_value_weight[layer_number], 'dp', axis=0, tiled=...  118 us
    all_gather x2, waiting for transfers between devices, fetch_weights(): lax.all_gather(feedforward_out_weight[layer_number], 'dp', axis=0, tiled=...  104 us
    all_gather x2, waiting for transfers between devices, fetch_weights(): lax.all_gather(feedforward_in_weight[layer_number], 'dp', axis=0, tiled=T...  96 us
    all_to_all x4, waiting for transfers between devices, layer_forward(): lax.all_to_all(mixture_h, 'sp', split_axis=1, concat_axis=2, tiled=True)  30 us
    dot_general x2, matrix products, layer_backward(): jnp.einsum('stf,df->std', grad_pre, feedforward_in_weight, preferred_elem...  24.1 us
    all_to_all x2, waiting for transfers between devices, layer_forward(): lax.all_to_all(query_rows, 'sp', split_axis=2, concat_axis=1, tiled=True)  24.1 us
    dot_general x2, matrix products, layer_forward(): jnp.einsum('stf,fd->std', activation, feedforward_out_weight, preferred_e...  23.5 us
  transfers between devices with their start and end apart: 27, of which 20 were waited for; matrix products, arithmetic and copies ran while one was open for 24% of the time, Pallas kernels for 0%

commit v1 on v0

--- a/solution.py
+++ b/solution.py
@@ -4,7 +4,9 @@
 import jax
 import jax.numpy as jnp
 from jax import lax
-from jax.sharding import PartitionSpec as P
+from jax.experimental import pallas as pl
+from jax.experimental.pallas import tpu as pltpu
+from jax.sharding import Mesh, PartitionSpec as P
 
 HEAD_SIZE = 64
 
@@ -13,6 +15,7 @@
 ADAPTER_ALPHA = 32.0
 EXACT_PRECISION = lax.Precision.HIGHEST
 MASKED = -1e30
+SP = ("z", "core")
 
 
 def layer_norm(tensor, gains, shifts):
@@ -29,16 +32,95 @@
     feedforward_out_weight,
     layer_number,
 ):
+    core = lax.axis_index("core")
+
+    def fetch(shards):
+        half = shards.shape[1] // 2
+        part = lax.dynamic_slice_in_dim(shards[layer_number], core * half, half, 0)
+        return lax.all_gather(part, ("dp", "core"), axis=0, tiled=True)
+
     return (
-        lax.all_gather(query_key_value_weight[layer_number], "dp", axis=0, tiled=True),
-        lax.all_gather(attention_out_weight[layer_number], "dp", axis=0, tiled=True),
-        lax.all_gather(feedforward_in_weight[layer_number], "dp", axis=0, tiled=True),
-        lax.all_gather(feedforward_out_weight[layer_number], "dp", axis=0, tiled=True),
-    )
+        fetch(query_key_value_weight),
+        fetch(attention_out_weight),
+        fetch(feedforward_in_weight),
+        fetch(feedforward_out_weight),
+    )
+
+
+def sum_kernel(sizes, terms_ref, out_ref, landing, send_sem, recv_sem, send_sem2, recv_sem2):
+    count = math.prod(sizes)
+    me = [lax.axis_index(name) for name in ("dp", "z", "core")]
+    mine = (me[0] * sizes[1] + me[1]) * sizes[2] + me[2]
+
+    def place(step):
+        other = lax.rem(mine + step, count)
+        return other, (
+            other // (sizes[1] * sizes[2]),
+            lax.rem(other // sizes[2], sizes[1]),
+            lax.rem(other, sizes[2]),
+        )
+
+    barrier = pltpu.get_barrier_semaphore()
+    for step in range(1, count):
+        pl.semaphore_signal(
+            barrier, inc=1, device_id=place(step)[1], device_id_type=pl.DeviceIdType.MESH
+        )
+    pl.semaphore_wait(barrier, count - 1)
+
+    def scatter(step):
+        other, device = place(step)
+        return pltpu.make_async_remote_copy(
+            src_ref=terms_ref.at[other],
+            dst_ref=landing.at[step],
+            send_sem=send_sem.at[step],
+            recv_sem=recv_sem.at[step],
+            device_id=device,
+            device_id_type=pl.DeviceIdType.MESH,
+        )
+
+    def spread(step):
+        other, device = place(step)
+        return pltpu.make_async_remote_copy(
+            src_ref=out_ref.at[mine],
+            dst_ref=out_ref.at[mine],
+            send_sem=send_sem2.at[step],
+            recv_sem=recv_sem2.at[step],
+            device_id=device,
+            device_id_type=pl.DeviceIdType.MESH,
+        )
+
+    for step in range(1, count):
+        scatter(step).start()
+    landing[0] = terms_ref[mine]
+    for step in range(1, count):
+        scatter(step).wait()
+    out_ref[mine] = jnp.sum(landing[...], axis=0)
+    for step in range(1, count):
+        spread(step).start()
+    for step in range(1, count):
+        spread(step).wait()
 
 
 def sum_adapters(down_terms, up_terms):
-    return lax.psum((down_terms, up_terms), ("dp", "sp"))
+    sizes = [lax.axis_size(name) for name in ("dp", "z", "core")]
+    count = math.prod(sizes)
+    packed = jnp.stack([down_terms, up_terms])
+    if count > 64 or packed.size % (count * 1024) != 0:
+        return lax.psum((down_terms, up_terms), ("dp", "z", "core"))
+    pieces = packed.reshape(count, -1, 128)
+    vmem = pl.BlockSpec(memory_space=pltpu.VMEM)
+    summed = pl.pallas_call(
+        partial(sum_kernel, sizes),
+        out_shape=jax.ShapeDtypeStruct(pieces.shape, jnp.float32),
+        in_specs=[vmem],
+        out_specs=vmem,
+        scratch_shapes=[pltpu.VMEM(pieces.shape, jnp.float32)]
+        + [pltpu.SemaphoreType.DMA((count,))] * 4,
+        name="adapter_sum",
+        compiler_params=pltpu.CompilerParams(collective_id=0, has_side_effects=True),
+    )(pieces)
+    summed = summed.reshape(packed.shape)
+    return summed[0], summed[1]
 
 
 def slot_scores(query_rows, key_rows, document_starts):
@@ -150,13 +232,11 @@
         + adapter_scale
         * jnp.einsum("wah,hp->wap", value_row_block, up_projection[1], precision=EXACT_PRECISION)
     ).astype(jnp.bfloat16)
-    queries_h, keys_h, values_h = (
-        lax.all_to_all(query_rows, "sp", split_axis=2, concat_axis=1, tiled=True),
-        lax.all_to_all(key_rows, "sp", split_axis=2, concat_axis=1, tiled=True),
-        lax.all_to_all(value_rows, "sp", split_axis=2, concat_axis=1, tiled=True),
+    queries_h, keys_h, values_h = lax.all_to_all(
+        jnp.stack([query_rows, key_rows, value_rows]), SP, split_axis=3, concat_axis=2, tiled=True
     )
     mixture_h, log_total = lax.map(slot_forward, (queries_h, keys_h, values_h, document_begin))
-    mixture = lax.all_to_all(mixture_h, "sp", split_axis=1, concat_axis=2, tiled=True)
+    mixture = lax.all_to_all(mixture_h, SP, split_axis=1, concat_axis=2, tiled=True)
     attended = hidden_state + (
         jnp.einsum("std,de->ste", mixture, attention_out_weight, preferred_element_type=jnp.float32)
         + attention_out_bias
@@ -235,14 +315,12 @@
         attention_out_weight,
         preferred_element_type=jnp.float32,
     ).astype(jnp.bfloat16)
-    grad_mixture_h = lax.all_to_all(grad_mixture, "sp", split_axis=2, concat_axis=1, tiled=True)
+    grad_mixture_h = lax.all_to_all(grad_mixture, SP, split_axis=2, concat_axis=1, tiled=True)
     grad_q_h, grad_k_h, grad_v_h = lax.map(
         slot_backward, (queries_h, keys_h, values_h, document_begin, log_total, grad_mixture_h)
     )
-    grad_queries, grad_keys, grad_values = (
-        lax.all_to_all(grad_q_h, "sp", split_axis=1, concat_axis=2, tiled=True),
-        lax.all_to_all(grad_k_h, "sp", split_axis=1, concat_axis=2, tiled=True),
-        lax.all_to_all(grad_v_h, "sp", split_axis=1, concat_axis=2, tiled=True),
+    grad_queries, grad_keys, grad_values = lax.all_to_all(
+        jnp.stack([grad_q_h, grad_k_h, grad_v_h]), SP, split_axis=2, concat_axis=3, tiled=True
     )
     grad_queries = grad_queries * jnp.asarray(HEAD_SIZE ** (-0.5), jnp.bfloat16)
     stacked = jnp.concatenate([grad_queries, grad_keys, grad_values], -1)
@@ -317,6 +395,7 @@
     hidden_state = first_layer_input.astype(jnp.float32)
     inputs = []
     gathered = []
+    kept = []
     for layer_number in range(layers):
         weight_set = fetch_weights(
             query_key_value_weight,
@@ -327,30 +406,21 @@
         )
         inputs.append(hidden_state)
         gathered.append(weight_set)
-        hidden_state, unused_state = layer_forward(
+        hidden_state, saved_state = layer_forward(
             hidden_state, weight_set, params_of(layer_number), document_begin
         )
+        kept.append(saved_state)
     gradient = cotangent.astype(jnp.float32)
     down_parts = [None] * layers
     up_parts = [None] * layers
     for layer_number in reversed(range(layers)):
-        weight_set = fetch_weights(
-            query_key_value_weight,
-            attention_out_weight,
-            feedforward_in_weight,
-            feedforward_out_weight,
-            layer_number,
-        )
-        unused_result, saved_state = layer_forward(
-            inputs[layer_number], weight_set, params_of(layer_number), document_begin
-        )
         gradient, down_terms, up_terms = layer_backward(
             inputs[layer_number],
             gradient,
-            weight_set,
+            gathered[layer_number],
             params_of(layer_number),
             document_begin,
-            saved_state,
+            kept[layer_number],
         )
         down_parts[layer_number] = down_terms
         up_parts[layer_number] = up_terms
@@ -361,16 +431,19 @@
         first_layer_input.shape[0]
         * first_layer_input.shape[1]
         * lax.axis_size("dp")
-        * lax.axis_size("sp")
+        * lax.axis_size("z")
+        * lax.axis_size("core")
     )
     token_scale = 1.0 / math.sqrt(tokens)
     return (hidden_state, gradient, grad_down * token_scale, grad_up * token_scale)
 
 
 def solution(mesh):
+    rows, columns = mesh.devices.shape
+    mesh = Mesh(mesh.devices.reshape(rows, columns // 2, 2), ("dp",) + SP)
     placed = (
-        P("dp", "sp", None),
-        P("dp", "sp", None),
+        P("dp", SP, None),
+        P("dp", SP, None),
         P("dp", None),
         P(None, "dp", None),
         P(None, "dp", None),
@@ -389,6 +462,6 @@
         body,
         mesh=mesh,
         in_specs=placed,
-        out_specs=(P("dp", "sp", None), P("dp", "sp", None), P(), P()),
+        out_specs=(P("dp", SP, None), P("dp", SP, None), P(), P()),
         check_vma=False,
     )

time: 1030 us -> 684 us (0.66)
  waiting for transfers between devices: 582 us -> 279 us
  blocking collectives: 0 us -> 78.8 us
  starting transfers between devices: 79.7 us -> 23.2 us
  local copies, waits for them, and re-layouts: 114 us -> 72.3 us
  matrix products: 183 us -> 152 us
  Pallas kernels: 0 us -> 16.2 us
  other arithmetic: 48.3 us -> 37.9 us
    all_gather x8, waiting for transfers between devices: 318 us -> 149 us  [fetch(): return lax.all_gather(part, ('dp', 'core'), axis=0, tiled=True)]
    psum x1 -> x0, waiting for transfers between devices: 118 us -> none  [sum_adapters(): return lax.psum((down_terms, up_terms), ('dp', 'sp'))]
    all_to_all x0 -> x3, blocking collectives: none -> 78.8 us  [the longest x1 40.5 us: layer_backward(): lax.all_to_all(jnp.stack([grad_q_h, grad_k_h, grad_v_h]), SP, split_axis=...]
    all_to_all x18 -> x5, starting transfers between devices: 78.9 us -> 22.4 us  [the longest x2 9.45 us: layer_forward(): lax.all_to_all(jnp.stack([query_rows, key_rows, value_rows]), SP, split_a...]
    all_to_all x32 -> x10, local copies, waits for them, and re-layouts: 36.7 us -> 9.13 us  [the longest x2 3.44 us: layer_backward(): lax.all_to_all(jnp.stack([grad_q_h, grad_k_h, grad_v_h]), SP, split_axis=...]
    pallas_call x0 -> x1, Pallas kernels: none -> 16.2 us  [sum_adapters(): pl.pallas_call(partial(sum_kernel, sizes), out_shape=jax.ShapeDtypeStruct...]
    all_to_all x18 -> x5, waiting for transfers between devices: 144 us -> 131 us  [the longest x2 72.8 us: layer_forward(): lax.all_to_all(jnp.stack([query_rows, key_rows, value_rows]), SP, split_a...]
    another operation x12 -> x32, local copies, waits for them, and re-layouts: 7.57 us -> 19 us  [the longest x14 7.54 us: layer_forward(): queries_h, keys_h, values_h = lax.all_to_all(jnp.stack([query_rows, key_r...]
  transfers between devices with their start and end apart: 27 -> 13, of which waited for: 20 -> 9; matrix products, arithmetic and copies ran while one was open for 24% -> 17% of each run, Pallas kernels for 0% -> 0%
where the time goes in v1:
time: 684 us; the launch traced here: 677 us
  waiting for transfers between devices  279 us (41%)
  matrix products  152 us (22%)
  blocking collectives  78.8 us (12%)
  local copies, waits for them, and re-layouts  72.3 us (11%)
  other arithmetic  37.9 us (6%)
  starting transfers between devices  23.2 us (3%)
  Pallas kernels  16.2 us (2%)
  between operations  15.9 us (2%)
    all_gather x8, waiting for transfers between devices, fetch(): return lax.all_gather(part, ('dp', 'core'), axis=0, tiled=True)  149 us
    all_to_all x2, waiting for transfers between devices, layer_forward(): lax.all_to_all(jnp.stack([query_rows, key_rows, value_rows]), SP, split_a...  72.8 us
    all_to_all x1, blocking collectives, layer_backward(): lax.all_to_all(jnp.stack([grad_q_h, grad_k_h, grad_v_h]), SP, split_axis=...  40.5 us
    all_to_all x1, waiting for transfers between devices, layer_backward(): lax.all_to_all(jnp.stack([grad_q_h, grad_k_h, grad_v_h]), SP, split_axis=...  27.8 us
    dot_general x2, matrix products, layer_backward(): jnp.einsum('stf,df->std', grad_pre, feedforward_in_weight, preferred_elem...  22.5 us
    all_to_all x1, blocking collectives, layer_forward(): lax.all_to_all(mixture_h, SP, split_axis=1, concat_axis=2, tiled=True)  19.2 us
    all_to_all x1, blocking collectives, layer_backward(): lax.all_to_all(grad_mixture, SP, split_axis=2, concat_axis=1, tiled=True)  19.2 us
    dot_general x2, matrix products, layer_forward(): jnp.einsum('std,df->stf', normed_mlp, feedforward_in_weight, preferred_el...  16.9 us
  transfers between devices with their start and end apart: 13, of which 9 were waited for; matrix products, arithmetic and copies ran while one was open for 17% of the time, Pallas kernels for 0%

profile of v1, /device:TPU:0, one launch (start us, length us, event | category | flops | bytes accessed | tf_op | source)
XLA Modules:
  0.0 676.7 jit_solution(4038336661855204178)
XLA Ops:
  28.0 31.9 %all-gather.17.cloned.1.call-done = bf16[1,1024,3072]{2,1,0:T(8,128)(2,1)} async-done(((bf16[1,128,3072]{2,1,0:T(8,128)(2,1)}), bf16[1,1024,3072]{2,1,0:T(8,128)(2,1)}) %all-gather.17.cloned.1.call-update) | async-done | bytes 6291472 | tf_op jit(solution)/shard_map/all_gather | solution.py:40
  77.5 35.0 %all-to-all-done = bf16[3,2,128,1024]{2,1,0,3:T(2,128)(2,1)S(1)} async-done(((bf16[3,2,128,1024]{2,1,0,3:T(2,128)(2,1)}), bf16[3,2,128,1024]{2,1,0,3:T(2,128)(2,1)S(1)}, u32[]{:S(2)}, u32[]{:S(2)}) %all-to-all-start) | async-done | bytes 1572896 | tf_op jit(solution)/shard_map/all_to_all | solution.py:235
  115.6 12.9 %while.52 = (s32[]{:T(128)}, bf16[2,1024,128]{1,2,0:T(8,128)(2,1)S(1)}, f32[2,2,1024]{2,1,0:T(2,128)S(1)}, bf16[2,1024,128]{1,2,0:T(8,128)(2,1)S(1)}, s32[2,1024...) while((s32[]{:T(128)}, ...), condition=%wide.region_5.6_spmd, body=%wide.region_2.5_spmd.sunk | while | flops 556922880 | bytes 32583792 | solution.py:238
  134.1 14.6 %all-to-all-done.1 = bf16[2,1024,128]{2,0,1:T(2,128)(2,1)S(1)} async-done(((bf16[2,1024,128]{2,0,1:T(2,128)(2,1)}), bf16[2,1024,128]{2,0,1:T(2,128)(2,1)S(1)}, u32[]{:S(2)}, u32[]{:S(2)}) %all-to-all-start.1) | async-done | bytes 524320 | tf_op jit(solution)/shard_map/all_to_all | solution.py:239
  153.1 8.5 %fusion.55 = f32[2,128,4096]{2,1,0:T(8,128)} fusion(bf16[1,1024,4096]{2,1,0:T(8,128)(2,1)} %all-gather.21.cloned.1.call-done, f32[4096]{0:T(1024)S(1)} %bitcast.614, f32[2,128,1024]{2,1,0:T(8,128)S(1)} %get-tuple-element.331, f32[1024]{0:T(1024)S(1)} %bitcast.628, f32[1024]{0:T(1024)S(1)} %bitcast.623, f32[2,128]{1,0:T(2,128)S(1)} %fusion.232, ...), kind=kOutput, calls=%fused_computation.103 | convolution fusion | flops 2149842944 | bytes 13658112 | tf_op jit(solution)/shard_map/std,df->stf/dot_general | solution.py:246
  161.6 41.3 %all-gather.23.cloned.1.call-done = bf16[1,4096,1024]{2,1,0:T(8,128)(2,1)} async-done(((bf16[1,512,1024]{2,1,0:T(8,128)(2,1)}), bf16[1,4096,1024]{2,1,0:T(8,128)(2,1)}) %all-gather.23.cloned.1.call-update) | async-done | bytes 8388624 | tf_op jit(solution)/shard_map/all_gather | solution.py:40
  202.9 7.9 %fusion.277 = (f32[2,128]{1,0:T(2,128)S(1)}, f32[2,128,1024]{2,1,0:T(8,128)S(1)}) fusion(f32[2,128,1024]{2,1,0:T(8,128)} %copy-done.21, f32[1024]{0:T(1024)S(1)} %bitcast.617, bf16[1,4096,1024]{2,1,0:T(8,128)(2,1)} %all-gather.23.cloned.1.call-done, f32[2,128,4096]{2,1,0:T(8,128)} %fusion.55), kind=kOutput, calls=%fused_computation.373 | convolution fusion | flops 2157707008 | bytes 14685184 | tf_op jit(solution)/shard_map/stf,fd->std/dot_general | solution.py:253
  212.2 38.0 %all-gather.25.cloned.1.call-done = bf16[1,1024,3072]{2,1,0:T(8,128)(2,1)} async-done(((bf16[1,128,3072]{2,1,0:T(8,128)(2,1)}), bf16[1,1024,3072]{2,1,0:T(8,128)(2,1)}) %all-gather.25.cloned.1.call-update) | async-done | bytes 6291472 | tf_op jit(solution)/shard_map/all_gather | solution.py:40
  260.7 4.8 all-to-all-start.2
  265.6 37.8 %all-to-all-done.2 = bf16[3,2,128,1024]{2,1,0,3:T(2,128)(2,1)S(1)} async-done(((bf16[3,2,128,1024]{2,1,0,3:T(2,128)(2,1)}), bf16[3,2,128,1024]{2,1,0,3:T(2,128)(2,1)S(1)}, u32[]{:S(2)}, u32[]{:S(2)}) %all-to-all-start.2) | async-done | bytes 1572896 | tf_op jit(solution)/shard_map/all_to_all | solution.py:235
  308.1 12.9 %while.53 = (s32[]{:T(128)}, bf16[2,1024,128]{1,2,0:T(8,128)(2,1)S(1)}, f32[2,2,1024]{2,1,0:T(2,128)S(1)}, bf16[2,1024,128]{1,2,0:T(8,128)(2,1)S(1)}, s32[2,1024...) while((s32[]{:T(128)}, ...), condition=%wide.region_13.14_spmd, body=%wide.region_10.13_spmd.sunk | while | flops 556922880 | bytes 32583792 | solution.py:238
  322.1 19.2 %all_to_all.132 = bf16[2,1024,128]{2,0,1:T(2,128)(2,1)S(1)} all-to-all(bf16[2,1024,128]{2,0,1:T(2,128)(2,1)} %copy.58), channel_id=1, replica_groups=mesh['dp'=4,'z'=4,'core'=2] {'z','core'}, dimensions={1} | all-to-all | bytes 1048576 | tf_op jit(solution)/shard_map/all_to_all | solution.py:239
  346.5 8.5 %fusion.58 = f32[2,128,4096]{2,1,0:T(8,128)} fusion(bf16[1,1024,4096]{2,1,0:T(8,128)(2,1)} %all-gather.29.cloned.1.call-done, f32[4096]{0:T(1024)S(1)} %bitcast.613, f32[2,128,1024]{2,1,0:T(8,128)} %copy-done.12, f32[1024]{0:T(1024)S(1)} %bitcast.627, f32[1024]{0:T(1024)S(1)} %bitcast.625, f32[2,128]{1,0:T(2,128)S(1)} %fusion.234, ...), kind=kOutput, calls=%fused_computation.104 | convolution fusion | flops 2149842944 | bytes 13658112 | tf_op jit(solution)/shard_map/std,df->stf/dot_general | solution.py:246
  354.9 37.5 %all-gather.31.cloned.1.call-done = bf16[1,4096,1024]{2,1,0:T(8,128)(2,1)} async-done(((bf16[1,512,1024]{2,1,0:T(8,128)(2,1)}), bf16[1,4096,1024]{2,1,0:T(8,128)(2,1)}) %all-gather.31.cloned.1.call-update) | async-done | bytes 8388624 | tf_op jit(solution)/shard_map/all_gather | solution.py:40
  392.5 11.6 %multiply_reduce_fusion.4 = (f32[2,128]{1,0:T(2,128)S(1)}, f32[2,128,1024]{2,1,0:T(8,128)}) fusion(f32[2,128,1024]{2,1,0:T(8,128)S(1)} %copy-done.13, f32[2,128]{1,0:T(2,128)S(1)} %broadcast_multiply_fusion, f32[1024]{0:T(1024)S(1)} %bitcast.626, bf16[1,1024,4096]{2,1,0:T(8,128)(2,1)} %all-gather.29.cloned.1.call-done, f32[2,128,4096]{2,1,0:T(8,128)} %fusion.58, ...), kind=kOutput, calls=%fused_computation.236 | convolution fusion | flops 4316987392 | bytes 23599104 | tf_op jit(solution)/shard_map/stf,df->std/dot_general | solution.py:305
  415.0 15.3 %all-to-all-done.4 = bf16[2,128,1024]{1,0,2:T(2,128)(2,1)S(1)} async-done(((bf16[2,128,1024]{1,0,2:T(2,128)(2,1)}), bf16[2,128,1024]{1,0,2:T(2,128)(2,1)S(1)}, u32[]{:S(2)}, u32[]{:S(2)}) %all-to-all-start.4) | async-done | bytes 524320 | tf_op jit(solution)/shard_map/all_to_all | solution.py:318
  431.9 26.3 %while.54 = (s32[]{:T(128)}, bf16[2,1024,128]{1,2,0:T(8,128)(2,1)S(1)}, bf16[2,1024,128]{1,2,0:T(8,128)(2,1)S(1)}, bf16[2,1024,128]{1,2,0:T(8,128)(2,1)}, bf16[2...) while((s32[]{:T(128)}, ...), condition=%wide.region_20.21_spmd, body=%wide.region_18.20_spmd.sunk | while | flops 1370880000 | bytes 77664456 | solution.py:319
  462.8 40.5 %all_to_all.133 = bf16[3,2,1024,128]{3,1,0,2:T(2,128)(2,1)S(1)} all-to-all(bf16[3,2,1024,128]{3,1,0,2:T(2,128)(2,1)S(1)} %pad_maximum_fusion.2), channel_id=1, replica_groups=mesh['dp'=4,'z'=4,'core'=2] {'z','core'}, dimensions={2} | all-to-all | bytes 3145728 | tf_op jit(solution)/shard_map/all_to_all | solution.py:322
  514.6 11.0 %multiply_reduce_fusion.2 = (f32[2,128]{1,0:T(2,128)S(1)}, f32[2,128,1024]{2,1,0:T(8,128)S(1)}) fusion(f32[2,128,1024]{2,1,0:T(8,128)S(1)} %copy-done.22, f32[2,128]{1,0:T(2,128)S(1)} %copy-done.72, f32[1024]{0:T(1024)S(1)} %bitcast.624, bf16[1,1024,4096]{2,1,0:T(8,128)(2,1)} %all-gather.21.cloned.1.call-done, f32[2,128,4096]{2,1,0:T(8,128)} %fusion.55, ...), kind=kOutput, calls=%fused_computation.232 | convolution fusion | flops 4317249536 | bytes 24123392 | tf_op jit(solution)/shard_map/stf,df->std/dot_general | solution.py:305
  530.0 19.2 %all_to_all.134 = bf16[2,128,1024]{1,0,2:T(2,128)(2,1)S(1)} all-to-all(bf16[2,128,1024]{1,0,2:T(2,128)(2,1)} %copy.67), channel_id=1, replica_groups=mesh['dp'=4,'z'=4,'core'=2] {'z','core'}, dimensions={2} | all-to-all | bytes 1048576 | tf_op jit(solution)/shard_map/all_to_all | solution.py:318
  554.1 27.1 %while.55 = (s32[]{:T(128)}, bf16[2,1024,128]{1,2,0:T(8,128)(2,1)}, bf16[2,1024,128]{1,2,0:T(8,128)(2,1)}, bf16[2,1024,128]{1,2,0:T(8,128)(2,1)}, bf16[2,1024,12...) while((s32[]{:T(128)}, bf16[2,1024,128]{1,2,0:T(8,128)(2,1)}, ...), condition=%wide.region_27.28_spmd, body=%wide.region_25.27_spmd.sunk | while | flops 1370880000 | bytes 86053176 | solution.py:319
  595.0 8.5 %fusion.140 = f32[2,128,1024]{2,1,0:T(8,128)} fusion(f32[2,128,1024]{2,1,0:T(8,128)S(1)} %copy-done.14, bf16[1,4096,1024]{2,1,0:T(8,128)(2,1)} %all-gather.31.cloned.1.call-done, f32[2,128,4096]{2,1,0:T(8,128)} %fusion.58, f32[1024]{0:T(1024)S(1)} %bitcast.615), kind=kOutput, calls=%fused_computation.187 | convolution fusion | flops 2157445120 | bytes 14684160 | tf_op jit(solution)/shard_map/stf,fd->std/dot_general | solution.py:253
  604.8 27.8 %all-to-all-done.7 = bf16[3,2,1024,128]{3,1,0,2:T(2,128)(2,1)} async-done(((bf16[3,2,1024,128]{3,1,0,2:T(2,128)(2,1)}), bf16[3,2,1024,128]{3,1,0,2:T(2,128)(2,1)}, u32[]{:S(2)}, u32[]{:S(2)}) %all-to-all-start.7) | async-done | bytes 1572896 | tf_op jit(solution)/shard_map/all_to_all | solution.py:322
  651.2 16.2 %adapter_sum.1 = f32[32,8,128]{2,1,0:T(8,128)} custom-call(f32[32,8,128]{2,1,0:T(8,128)} %reshape.590.terms_ref), custom_call_target="tpu_custom_call" | custom-call | tf_op jit(solution)/shard_map/adapter_sum/pallas_call | solution.py:112
  (455 shorter events, 225.0 us)
Async XLA Ops:
  7.2 52.7 %all-gather.17.cloned.1.call-start = ((), (), s32[]{:S(2)}) async-start(), calls=%async_computation.8 | async-start | bytes 7077888 | tf_op jit(solution)/shard_map/all_gather | solution.py:40
  11.5 138.6 %all-gather.19.cloned.1.call-start = ((), (), s32[]{:S(2)}) async-start(), calls=%async_computation.9 | async-start | bytes 2359296 | tf_op jit(solution)/shard_map/all_gather | solution.py:40
  12.4 140.6 %all-gather.21.cloned.1.call-start = ((), (), s32[]{:S(2)}) async-start(), calls=%async_computation.10 | async-start | bytes 9437184 | tf_op jit(solution)/shard_map/all_gather | solution.py:40
  16.2 186.7 %all-gather.23.cloned.1.call-start = ((), (), s32[]{:S(2)}) async-start(), calls=%async_computation.11 | async-start | bytes 9437184 | tf_op jit(solution)/shard_map/all_gather | solution.py:40
  21.3 228.9 %all-gather.25.cloned.1.call-start = ((), (), s32[]{:S(2)}) async-start(), calls=%async_computation.12 | async-start | bytes 7077888 | tf_op jit(solution)/shard_map/all_gather | solution.py:40
  23.7 318.9 %all-gather.27.cloned.1.call-start = ((), (), s32[]{:S(2)}) async-start(), calls=%async_computation.13 | async-start | bytes 2359296 | tf_op jit(solution)/shard_map/all_gather | solution.py:40
  24.5 321.9 %all-gather.29.cloned.1.call-start = ((), (), s32[]{:S(2)}) async-start(), calls=%async_computation.14 | async-start | bytes 9437184 | tf_op jit(solution)/shard_map/all_gather | solution.py:40
  25.8 38.8 %copy-start.54 = (f32[2,128]{1,0:T(2,128)}, f32[2,128]{1,0:T(2,128)S(1)}, u32[]{:S(2)}) copy-start(f32[2,128]{1,0:T(2,128)S(1)} %broadcast_multiply_fusion.3) | copy-start | bytes 3076
  26.1 38.5 %copy-start.67 = (f32[2,128]{1,0:T(2,128)}, f32[2,128]{1,0:T(2,128)S(1)}, u32[]{:S(2)}) copy-start(f32[2,128]{1,0:T(2,128)S(1)} %fusion.231) | copy-start | bytes 3076
  26.2 126.9 %copy-start.84 = (f32[1,1,1024]{2,1,0:T(1,128)}, f32[1,1,1024]{2,1,0:T(1,128)S(1)}, u32[]{:S(2)}) copy-start(f32[1,1,1024]{2,1,0:T(1,128)S(1)} %get-tuple-element.315) | copy-start | bytes 12292
  26.2 184.8 %copy-start.49 = (f32[1,1,1024]{2,1,0:T(1,128)}, f32[1,1,1024]{2,1,0:T(1,128)S(1)}, u32[]{:S(2)}) copy-start(f32[1,1,1024]{2,1,0:T(1,128)S(1)} %get-tuple-element.317) | copy-start | bytes 12292
  70.1 42.4 %all-to-all-start = ((bf16[3,2,128,1024]{2,1,0,3:T(2,128)(2,1)}), bf16[3,2,128,1024]{2,1,0,3:T(2,128)(2,1)S(1)}, u32[]{:S(2)}, u32[]{:S(2)}) async-start(bf16[3,2,128,1024]{2,1,0,3:T(2,128)(2,1)} %copy.48), calls=%async_computation | async-start | bytes 3145728 | tf_op jit(solution)/shard_map/all_to_all | solution.py:235
  74.7 317.8 %all-gather.31.cloned.1.call-start = ((), (), s32[]{:S(2)}) async-start(), calls=%async_computation.15 | async-start | bytes 9437184 | tf_op jit(solution)/shard_map/all_gather | solution.py:40
  129.8 18.9 %all-to-all-start.1 = ((bf16[2,1024,128]{2,0,1:T(2,128)(2,1)}), bf16[2,1024,128]{2,0,1:T(2,128)(2,1)S(1)}, u32[]{:S(2)}, u32[]{:S(2)}) async-start(bf16[2,1024,128]{2,0,1:T(2,128)(2,1)} %copy.52), calls=%async_computation.1 | async-start | bytes 1048576 | tf_op jit(solution)/shard_map/all_to_all | solution.py:239
  210.8 131.8 %copy-start = (f32[2,128,1024]{2,1,0:T(8,128)}, f32[2,128,1024]{2,1,0:T(8,128)S(1)}, u32[]{:S(2)}) copy-start(f32[2,128,1024]{2,1,0:T(8,128)S(1)} %get-tuple-element.333) | copy-start | bytes 3145732
  211.0 43.7 %copy-start.75 = (f32[2,128]{1,0:T(2,128)}, f32[2,128]{1,0:T(2,128)S(1)}, u32[]{:S(2)}) copy-start(f32[2,128]{1,0:T(2,128)S(1)} %multiply_reduce_fusion.6) | copy-start | bytes 3076
  211.1 43.7 %copy-start.60 = (f32[2,128]{1,0:T(2,128)}, f32[2,128]{1,0:T(2,128)S(1)}, u32[]{:S(2)}) copy-start(f32[2,128]{1,0:T(2,128)S(1)} %fusion.233) | copy-start | bytes 3076
  211.7 44.2 %copy-start.2 = (bf16[2,128,1024]{2,1,0:T(8,128)(2,1)}, bf16[2,128,1024]{2,1,0:T(8,128)(2,1)S(1)}, u32[]{:S(2)}) copy-start(bf16[2,128,1024]{2,1,0:T(8,128)(2,1)S(1)} %add_convert_fusion.1) | copy-start | bytes 1572868
  212.2 42.6 %copy-start.45 = (f32[2,128,4]{1,2,0:T(4,128)}, f32[2,128,4]{1,2,0:T(4,128)S(1)}, u32[]{:S(2)}) copy-start(f32[2,128,4]{1,2,0:T(4,128)S(1)} %fusion.206) | copy-start | bytes 12292
  260.7 42.6 %all-to-all-start.2 = ((bf16[3,2,128,1024]{2,1,0,3:T(2,128)(2,1)}), bf16[3,2,128,1024]{2,1,0,3:T(2,128)(2,1)S(1)}, u32[]{:S(2)}, u32[]{:S(2)}) async-start(bf16[3,2,128,1024]{2,1,0,3:T(2,128)(2,1)} %copy.54), calls=%async_computation.2 | async-start | bytes 3145728 | tf_op jit(solution)/shard_map/all_to_all | solution.py:235
  346.4 46.0 %copy-start.13 = (f32[2,128,1024]{2,1,0:T(8,128)S(1)}, f32[2,128,1024]{2,1,0:T(8,128)}, u32[]{:S(2)}) copy-start(f32[2,128,1024]{2,1,0:T(8,128)} %copy-done.12) | copy-start | bytes 3145732
  346.5 46.0 %copy-start.35 = (bf16[2,128,1024]{2,1,0:T(8,128)(2,1)S(1)}, bf16[2,128,1024]{2,1,0:T(8,128)(2,1)}, u32[]{:S(2)}) copy-start(bf16[2,128,1024]{2,1,0:T(8,128)(2,1)} %param.24) | copy-start | bytes 1572868
  410.2 20.1 %all-to-all-start.4 = ((bf16[2,128,1024]{1,0,2:T(2,128)(2,1)}), bf16[2,128,1024]{1,0,2:T(2,128)(2,1)S(1)}, u32[]{:S(2)}, u32[]{:S(2)}) async-start(bf16[2,128,1024]{1,0,2:T(2,128)(2,1)} %copy.61), calls=%async_computation.4 | async-start | bytes 1048576 | tf_op jit(solution)/shard_map/all_to_all | solution.py:318
  590.5 42.1 %all-to-all-start.7 = ((bf16[3,2,1024,128]{3,1,0,2:T(2,128)(2,1)}), bf16[3,2,1024,128]{3,1,0,2:T(2,128)(2,1)}, u32[]{:S(2)}, u32[]{:S(2)}) async-start(bf16[3,2,1024,128]{3,1,0,2:T(2,128)(2,1)} %pad_maximum_fusion.3), calls=%async_computation.7 | async-start | bytes 3145728 | tf_op jit(solution)/shard_map/all_to_all | solution.py:322
  (83 other events, 791.5 us)
Sparse Core Ops, SparseCore 0:
  11.6 48.2 all-gather.16
  61.8 27.8 all-gather.18
  91.6 54.3 all-gather.20
  148.4 54.4 all-gather.22
  204.6 45.5 all-gather.24
  251.9 27.8 all-gather.26
  281.7 54.3 all-gather.28
  338.0 54.3 all-gather.30

commit v2 on v1

--- a/solution.py
+++ b/solution.py
@@ -438,30 +438,1002 @@
     return (hidden_state, gradient, grad_down * token_scale, grad_up * token_scale)
 
 
+MESH = pl.DeviceIdType.MESH
+BLOCK = 256
+TILE = 512
+VMEM_LIMIT = 60 * 1024 * 1024
+
+
+def dot_nn(left, right):
+    return jnp.dot(left, right, preferred_element_type=jnp.float32)
+
+
+def dot_nt(left, right):
+    return lax.dot_general(
+        left, right, (((1,), (1,)), ((), ())), preferred_element_type=jnp.float32
+    )
+
+
+def dot_tn(left, right):
+    return lax.dot_general(
+        left, right, (((0,), (0,)), ((), ())), preferred_element_type=jnp.float32
+    )
+
+
+def normalize(tensor):
+    centred = tensor - jnp.mean(tensor, -1, keepdims=True)
+    spread = jnp.mean(centred * centred, -1, keepdims=True)
+    scale = lax.rsqrt(spread + EPSILON)
+    return centred * scale, scale
+
+
+def norm_backward(tensor, gains, gradient):
+    unit, scale = normalize(tensor)
+    weighted = gradient * gains
+    first = jnp.mean(weighted, -1, keepdims=True)
+    second = jnp.mean(weighted * unit, -1, keepdims=True)
+    return scale * (weighted - first - unit * second)
+
+
+GELU_INNER = math.sqrt(2.0 / math.pi)
+GELU_CUBE = 0.044715
+
+
+def gelu(value):
+    inner = GELU_INNER * (value + GELU_CUBE * (value * value * value))
+    return 0.5 * value * (1.0 + jnp.tanh(inner))
+
+
+def gelu_slope(value):
+    square = value * value
+    bend = jnp.tanh(GELU_INNER * (value + GELU_CUBE * (square * value)))
+    climb = GELU_INNER * (1.0 + 3.0 * GELU_CUBE * square)
+    return 0.5 * (1.0 + bend) + 0.5 * value * (1.0 - bend * bend) * climb
+
+
+def split_heads(rows):
+    heads = rows.shape[1] // HEAD_SIZE
+    owner = lax.broadcasted_iota(jnp.int32, rows.shape, 1) // HEAD_SIZE
+    return jnp.concatenate(
+        [jnp.where(owner == head, rows, jnp.zeros_like(rows)) for head in range(heads)], 0
+    )
+
+
+def join_heads(stacked, length):
+    heads = stacked.shape[1] // HEAD_SIZE
+    owner = lax.broadcasted_iota(jnp.int32, (length, stacked.shape[1]), 1) // HEAD_SIZE
+    joined = stacked[:length]
+    for head in range(1, heads):
+        joined = jnp.where(owner == head, stacked[head * length : (head + 1) * length], joined)
+    return joined
+
+
+def allowed_pairs(key_block, query_block, begin_row, heads):
+    shape = (BLOCK, heads * BLOCK)
+    key_place = key_block * BLOCK + lax.broadcasted_iota(jnp.int32, shape, 0)
+    column = lax.broadcasted_iota(jnp.int32, (1, heads * BLOCK), 1)
+    query_place = query_block * BLOCK + lax.rem(column, BLOCK)
+    return (key_place >= begin_row) & (key_place <= query_place)
+
+
+def greet(peers):
+    barrier = pltpu.get_barrier_semaphore()
+    for peer in peers:
+        pl.semaphore_signal(barrier, inc=1, device_id=peer, device_id_type=MESH)
+    pl.semaphore_wait(barrier, len(peers))
+
+
+def remote(source, target, send_sem, recv_sem, device):
+    return pltpu.make_async_remote_copy(
+        src_ref=source,
+        dst_ref=target,
+        send_sem=send_sem,
+        recv_sem=recv_sem,
+        device_id=device,
+        device_id_type=MESH,
+    )
+
+
+def stream(count, copies, body):
+    for copy in copies(0, 0):
+        copy.start()
+
+    def step(index, carry):
+        slot = lax.rem(index, 2)
+
+        @pl.when(index + 1 < count)
+        def _():
+            for copy in copies(index + 1, 1 - slot):
+                copy.start()
+
+        for copy in copies(index, slot):
+            copy.wait()
+        body(index, slot)
+        return carry
+
+    lax.fori_loop(0, count, step, 0)
+
+
+def at_columns(index, size):
+    return pl.ds(pl.multiple_of(index * size, size), size)
+
+
+class Gather:
+    def __init__(self, shard, full, shards, chip, lane, sems):
+        self.shard, self.full = shard, full
+        self.rows = shard.shape[0]
+        self.chip, self.core = chip, lax.rem(lane, 2)
+        self.next_x = chip + 1 - 2 * lax.rem(chip, 2)
+        self.next_y = lax.rem(chip + 2, shards)
+        self.far = shards - 1 - chip
+        self.to_x, self.to_y = (self.next_x, lane), (self.next_y, lane)
+        self.to_core = (chip, lane + 1 - 2 * self.core)
+        self.send_sem, self.recv_sem, self.core_send, self.core_recv, self.own_sem = sems
+
+    def quarter(self, owner, part):
+        size = self.rows // 4
+        start = self.core * (2 * size) + part * size
+        if owner is None:
+            return self.shard.at[pl.ds(pl.multiple_of(start, size), size)]
+        return self.full.at[pl.ds(pl.multiple_of(owner * self.rows + start, size), size)]
+
+    def hop(self, index):
+        source, owner, part, device = (
+            (None, self.chip, 0, self.to_x),
+            (None, self.chip, 1, self.to_y),
+            (None, self.chip, 0, self.to_y),
+            (None, self.chip, 1, self.to_x),
+            (self.next_x, self.next_x, 0, self.to_y),
+            (self.next_y, self.next_y, 1, self.to_x),
+        )[index]
+        return remote(
+            self.quarter(source, part),
+            self.quarter(owner, part),
+            self.send_sem.at[index],
+            self.recv_sem.at[index],
+            device,
+        )
+
+    def across(self, index):
+        owner = (self.next_x, self.next_y, self.far)[index]
+        size = self.rows // 2
+        start = pl.multiple_of(owner * self.rows + self.core * size, size)
+        half = self.full.at[pl.ds(start, size)]
+        return remote(
+            half, half, self.core_send.at[index], self.core_recv.at[index], self.to_core
+        )
+
+    def own(self):
+        start = pl.multiple_of(self.chip * self.rows, self.rows)
+        return pltpu.make_async_copy(
+            self.shard, self.full.at[pl.ds(start, self.rows)], self.own_sem
+        )
+
+    def begin(self):
+        for index in range(4):
+            self.hop(index).start()
+
+    def pass_on(self):
+        self.hop(0).wait_recv()
+        self.hop(4).start()
+        self.hop(1).wait_recv()
+        self.hop(5).start()
+
+    def cross(self):
+        self.hop(3).wait_recv()
+        self.across(0).start()
+        self.hop(2).wait_recv()
+        self.across(1).start()
+        self.hop(4).wait_recv()
+        self.hop(5).wait_recv()
+        self.across(2).start()
+
+    def arrive(self):
+        for index in range(3):
+            self.across(index).wait_recv()
+        self.own().wait()
+
+    def drain(self):
+        for index in range(6):
+            self.hop(index).wait_send()
+        for index in range(3):
+            self.across(index).wait_send()
+
+
+def forward_kernel(
+    layer,
+    sizes,
+    hidden,
+    begin,
+    shard_qkv,
+    shard_out,
+    shard_in,
+    shard_back,
+    qkv_bias,
+    out_bias,
+    in_bias,
+    back_bias,
+    gains,
+    shifts,
+    down,
+    up,
+    result,
+    normed,
+    low_rank,
+    heads_in,
+    mixed,
+    log_total,
+    attended,
+    pre_act,
+    full_qkv,
+    full_out,
+    full_in,
+    full_back,
+    tile_in,
+    tile_back,
+    out_weight,
+    heads_out,
+    mixture,
+    scores,
+    activation,
+    total,
+    tile_sem,
+    out_sem,
+    heads_send,
+    heads_recv,
+    mix_send,
+    mix_recv,
+    hop_send,
+    hop_recv,
+    core_send,
+    core_recv,
+    own_sem,
+):
+    chips, lanes = sizes
+    chip, lane = lax.axis_index("dp"), lax.axis_index("sp")
+    slots, length, width = heads_in.shape[2:]
+    heads = width // HEAD_SIZE
+    rows, model = hidden.shape
+    hidden_units = in_bias.shape[1]
+    blocks = lanes * length // BLOCK
+    per_block = BLOCK // length
+
+    def others():
+        return [lax.rem(lane + step, lanes) for step in range(1, lanes)]
+
+    gathers = [
+        Gather(
+            shard.at[layer],
+            full,
+            chips,
+            chip,
+            lane,
+            (
+                hop_send.at[index],
+                hop_recv.at[index],
+                core_send.at[index],
+                core_recv.at[index],
+                own_sem.at[index],
+            ),
+        )
+        for index, (shard, full) in enumerate(
+            (
+                (shard_qkv, full_qkv),
+                (shard_out, full_out),
+                (shard_in, full_in),
+                (shard_back, full_back),
+            )
+        )
+    ]
+    get_qkv, get_out, get_in, get_back = gathers
+    greet([(chip, other) for other in others()] + [get_qkv.to_x, get_qkv.to_y])
+    get_qkv.begin()
+    for gather in gathers:
+        gather.own().start()
+
+    unit, _ = normalize(hidden[...])
+    normed[...] = (unit * gains[0:1] + shifts[0:1]).astype(jnp.bfloat16)
+    low_rank[...] = dot_nt(normed[...], down[...])
+    get_qkv.pass_on()
+    get_out.begin()
+    get_in.begin()
+    get_qkv.cross()
+    get_qkv.arrive()
+
+    def qkv_tile(index, slot):
+        return [
+            pltpu.make_async_copy(
+                full_qkv.at[:, at_columns(index, TILE)], tile_in.at[slot], tile_sem.at[0, slot]
+            )
+        ]
+
+    per_tile = TILE // width
+    tiles_each = model // TILE
+
+    def qkv_body(index, slot):
+        columns = at_columns(index, TILE)
+        value = dot_nn(normed[...], tile_in[slot])
+        value += dot_nn(low_rank[...].astype(jnp.bfloat16), up[:, columns])
+        value += qkv_bias[0:1, columns]
+        value = (value * qkv_bias[1:2, columns]).astype(jnp.bfloat16)
+        kind = index // tiles_each
+        first = lax.rem(index, tiles_each) * per_tile
+        for step in range(per_tile):
+            part = value[:, step * width : (step + 1) * width]
+            for slot_at in range(slots):
+                heads_out[slot_at, first + step, kind] = part[
+                    slot_at * length : (slot_at + 1) * length
+                ]
+
+    stream(3 * tiles_each, qkv_tile, qkv_body)
+
+    def send_heads(slot_at, other):
+        return remote(
+            heads_out.at[slot_at, other],
+            heads_in.at[lane, :, slot_at],
+            heads_send.at[slot_at, other],
+            heads_recv.at[slot_at, lane],
+            (chip, other),
+        )
+
+    def take_heads(slot_at, other):
+        return remote(
+            heads_out.at[slot_at, other],
+            heads_in.at[other, :, slot_at],
+            heads_send.at[slot_at, other],
+            heads_recv.at[slot_at, other],
+            (chip, other),
+        )
+
+    for slot_at in range(slots):
+        for other in others():
+            send_heads(slot_at, other).start()
+        heads_in[lane, :, slot_at] = heads_out[slot_at, lane]
+
+    get_out.pass_on()
+    get_in.pass_on()
+    get_back.begin()
+
+    def send_mixed(slot_at, other):
+        return remote(
+            mixed.at[slot_at, other],
+            mixture.at[lane, slot_at],
+            mix_send.at[slot_at, other],
+            mix_recv.at[slot_at, lane],
+            (chip, other),
+        )
+
+    def take_mixed(slot_at, other):
+        return remote(
+            mixed.at[slot_at, other],
+            mixture.at[other, slot_at],
+            mix_send.at[slot_at, other],
+            mix_recv.at[slot_at, other],
+            (chip, other),
+        )
+
+    def attend(slot_at):
+        def token_rows(kind, block):
+            return heads_in[pl.ds(block * per_block, per_block), kind, slot_at].reshape(
+                BLOCK, width
+            )
+
+        def query_step(query_block, carry):
+            queries = split_heads(token_rows(0, query_block))
+            begin_row = begin[slot_at, query_block]
+
+            def score_step(key_block, best):
+                found = dot_nt(token_rows(1, key_block), queries)
+                open_pairs = allowed_pairs(key_block, query_block, begin_row, heads)
+                found = jnp.where(open_pairs, found, MASKED)
+                scores[key_block] = found
+                return jnp.maximum(best, jnp.max(found, 0, keepdims=True))
+
+            best = lax.fori_loop(
+                0, query_block + 1, score_step, jnp.full((1, heads * BLOCK), MASKED, jnp.float32)
+            )
+
+            def exp_step(key_block, sums):
+                raised = jnp.exp(scores[key_block] - best)
+                scores[key_block] = raised
+                return sums + jnp.sum(raised, 0, keepdims=True)
+
+            sums = lax.fori_loop(
+                0, query_block + 1, exp_step, jnp.zeros((1, heads * BLOCK), jnp.float32)
+            )
+            log_total[slot_at, query_block] = best + jnp.log(sums)
+            inverse = 1.0 / sums
+
+            def mix_step(key_block, mix):
+                weights = (scores[key_block] * inverse).astype(jnp.bfloat16)
+                return mix + dot_tn(weights, token_rows(2, key_block))
+
+            mix = lax.fori_loop(
+                0, query_block + 1, mix_step, jnp.zeros((heads * BLOCK, width), jnp.float32)
+            )
+            out = join_heads(mix, BLOCK).astype(jnp.bfloat16)
+            for part in range(per_block):
+                other = query_block * per_block + part
+                mixed[slot_at, other] = out[part * length : (part + 1) * length]
+
+                @pl.when(other != lane)
+                def _():
+                    send_mixed(slot_at, other).start()
+
+            return carry
+
+        lax.fori_loop(0, blocks, query_step, 0)
+
+    for slot_at in range(slots):
+        for other in others():
+            take_heads(slot_at, other).wait_recv()
+        attend(slot_at)
+        mixture[lane, slot_at] = mixed[slot_at, lane]
+        if slot_at == 0:
+            get_out.cross()
+            get_out.arrive()
+            pltpu.make_async_copy(full_out, out_weight, out_sem).start()
+
+    pltpu.make_async_copy(full_out, out_weight, out_sem).wait()
+    for slot_at in range(slots):
+        for other in others():
+            take_mixed(slot_at, other).wait_recv()
+    total[...] = hidden[...] + out_bias[...]
+
+    def out_body(index, carry):
+        part = jnp.concatenate(
+            [mixture[2 * index].reshape(rows, width), mixture[2 * index + 1].reshape(rows, width)],
+            1,
+        )
+        start = pl.multiple_of(index * 2 * width, 2 * width)
+        total[...] += dot_nn(part, out_weight[pl.ds(start, 2 * width)])
+        return carry
+
+    lax.fori_loop(0, lanes // 2, out_body, 0)
+    attended[...] = total[...]
+    unit, _ = normalize(total[...])
+    second = (unit * gains[1:2] + shifts[1:2]).astype(jnp.bfloat16)
+    get_in.cross()
+    get_in.arrive()
+
+    def in_tile(index, slot):
+        return [
+            pltpu.make_async_copy(
+                full_in.at[:, at_columns(index, TILE)], tile_in.at[slot], tile_sem.at[0, slot]
+            )
+        ]
+
+    def in_body(index, slot):
+        columns = at_columns(index, TILE)
+        value = dot_nn(second, tile_in[slot]) + in_bias[:, columns]
+        pre_act[:, columns] = value.astype(jnp.bfloat16)
+        activation[index] = gelu(value).astype(jnp.bfloat16)
+
+    get_back.pass_on()
+    stream(hidden_units // TILE, in_tile, in_body)
+    get_back.cross()
+    get_back.arrive()
+    total[...] += back_bias[...]
+
+    def back_tile(index, slot):
+        return [
+            pltpu.make_async_copy(
+                full_back.at[at_columns(index, TILE)], tile_back.at[slot], tile_sem.at[1, slot]
+            )
+        ]
+
+    def back_body(index, slot):
+        total[...] += dot_nn(activation[index], tile_back[slot])
+
+    stream(hidden_units // TILE, back_tile, back_body)
+    result[...] = total[...]
+    for gather in gathers:
+        gather.drain()
+    for slot_at in range(slots):
+        for other in others():
+            send_heads(slot_at, other).wait_send()
+            send_mixed(slot_at, other).wait_send()
+
+
+def backward_kernel(
+    sizes,
+    gradient,
+    hidden,
+    begin,
+    gains,
+    down,
+    up,
+    normed,
+    low_rank,
+    heads_in,
+    mixed,
+    log_total,
+    attended,
+    pre_act,
+    full_qkv,
+    full_out,
+    full_in,
+    full_back,
+    result,
+    adapters,
+    tile_in,
+    tile_back,
+    out_weight,
+    qkv_weight,
+    total,
+    grad_attended,
+    mix_out,
+    mix_in,
+    queries,
+    mix_heads,
+    delta,
+    query_sum,
+    key_sum,
+    value_sum,
+    heads_out,
+    grads_in,
+    grads_flat,
+    tile_sem,
+    load_sem,
+    mix_send,
+    mix_recv,
+    heads_send,
+    heads_recv,
+):
+    chips, lanes = sizes
+    chip, lane = lax.axis_index("dp"), lax.axis_index("sp")
+    slots, length, width = heads_in.shape[2:]
+    heads = width // HEAD_SIZE
+    rows, model = hidden.shape
+    hidden_units = pre_act.shape[1]
+    blocks = lanes * length // BLOCK
+    per_block = BLOCK // length
+
+    def others():
+        return [lax.rem(lane + step, lanes) for step in range(1, lanes)]
+
+    greet([(chip, other) for other in others()])
+    load_out = pltpu.make_async_copy(full_out, out_weight, load_sem.at[0])
+    load_qkv = pltpu.make_async_copy(full_qkv, qkv_weight, load_sem.at[1])
+
+    low_gradient = gradient[...].astype(jnp.bfloat16)
+    total[...] = jnp.zeros_like(total)
+
+    def tiles(index, slot):
+        part = at_columns(index, TILE)
+        return [
+            pltpu.make_async_copy(full_in.at[:, part], tile_in.at[slot], tile_sem.at[0, slot]),
+            pltpu.make_async_copy(full_back.at[part], tile_back.at[slot], tile_sem.at[1, slot]),
+        ]
+
+    def forward_tile(index, slot):
+        columns = at_columns(index, TILE)
+        grad_act = dot_nt(low_gradient, tile_back[slot])
+        slope = gelu_slope(pre_act[:, columns].astype(jnp.float32))
+        grad_pre = (slope * grad_act).astype(jnp.bfloat16)
+        total[...] += dot_nt(grad_pre, tile_in[slot])
+
+    stream(hidden_units // TILE, tiles, forward_tile)
+    load_out.start()
+    load_qkv.start()
+    grad_attended[...] = gradient[...] + norm_backward(attended[...], gains[1:2], total[...])
+    low_attended = grad_attended[...].astype(jnp.bfloat16)
+    load_out.wait()
+
+    def send_mix(slot_at, other):
+        return remote(
+            mix_out.at[slot_at, other],
+            mix_in.at[lane, slot_at],
+            mix_send.at[slot_at, other],
+            mix_recv.at[slot_at, lane],
+            (chip, other),
+        )
+
+    def take_mix(slot_at, other):
+        return remote(
+            mix_out.at[slot_at, other],
+            mix_in.at[other, slot_at],
+            mix_send.at[slot_at, other],
+            mix_recv.at[slot_at, other],
+            (chip, other),
+        )
+
+    def mix_body(index, carry):
+        start = pl.multiple_of(index * 2 * width, 2 * width)
+        value = dot_nt(low_attended, out_weight[pl.ds(start, 2 * width)]).astype(jnp.bfloat16)
+        for step in range(2):
+            part = value[:, step * width : (step + 1) * width]
+            for slot_at in range(slots):
+                mix_out[slot_at, 2 * index + step] = part[
+                    slot_at * length : (slot_at + 1) * length
+                ]
+        return carry
+
+    lax.fori_loop(0, lanes // 2, mix_body, 0)
+    for slot_at in range(slots):
+        for other in others():
+            send_mix(slot_at, other).start()
+        mix_in[lane, slot_at] = mix_out[slot_at, lane]
+
+    def send_heads(slot_at, other):
+        return remote(
+            heads_out.at[slot_at, other],
+            grads_in.at[lane, slot_at],
+            heads_send.at[slot_at, other],
+            heads_recv.at[slot_at, lane],
+            (chip, other),
+        )
+
+    def take_heads(slot_at, other):
+        return remote(
+            heads_out.at[slot_at, other],
+            grads_in.at[other, slot_at],
+            heads_send.at[slot_at, other],
+            heads_recv.at[slot_at, other],
+            (chip, other),
+        )
+
+    def attend(slot_at):
+        def token_rows(kind, block):
+            return heads_in[pl.ds(block * per_block, per_block), kind, slot_at].reshape(
+                BLOCK, width
+            )
+
+        def prepare(block, carry):
+            queries[block] = split_heads(token_rows(0, block))
+            grads = mix_in[pl.ds(block * per_block, per_block), slot_at].reshape(BLOCK, width)
+            grads = split_heads(grads)
+            mix_heads[block] = grads
+            mix = mixed[slot_at, pl.ds(block * per_block, per_block)].reshape(BLOCK, width)
+            mix = jnp.concatenate([mix] * heads, 0).astype(jnp.float32)
+            product = grads.astype(jnp.float32) * mix
+            delta[block] = jnp.sum(product.T, 0, keepdims=True)
+            query_sum[block] = jnp.zeros_like(query_sum[block])
+            return carry
+
+        lax.fori_loop(0, blocks, prepare, 0)
+
+        def key_step(key_block, carry):
+            keys = token_rows(1, key_block)
+            values = token_rows(2, key_block)
+            key_sum[...] = jnp.zeros_like(key_sum)
+            value_sum[...] = jnp.zeros_like(value_sum)
+
+            def query_step(query_block, inner):
+                query_heads = queries[query_block]
+                grad_heads = mix_heads[query_block]
+                found = dot_nt(keys, query_heads)
+                open_pairs = allowed_pairs(
+                    key_block, query_block, begin[slot_at, query_block], heads
+                )
+                weights = jnp.where(
+                    open_pairs, jnp.exp(found - log_total[slot_at, query_block]), 0.0
+                )
+                value_sum[...] += dot_nn(weights.astype(jnp.bfloat16), grad_heads)
+                grad_weights = dot_nt(values, grad_heads)
+                grad_scores = (weights * (grad_weights - delta[query_block])).astype(jnp.bfloat16)
+                key_sum[...] += dot_nn(grad_scores, query_heads)
+                query_sum[query_block] += dot_tn(grad_scores, keys)
+                return inner
+
+            lax.fori_loop(key_block, blocks, query_step, 0)
+            for kind, sums in ((1, key_sum), (2, value_sum)):
+                for part in range(per_block):
+                    heads_out[slot_at, key_block * per_block + part, kind] = sums[
+                        part * length : (part + 1) * length
+                    ].astype(jnp.bfloat16)
+            return carry
+
+        lax.fori_loop(0, blocks, key_step, 0)
+
+        def finish(block, carry):
+            out = join_heads(query_sum[block], BLOCK).astype(jnp.bfloat16)
+            out = out * jnp.asarray(HEAD_SIZE ** (-0.5), jnp.bfloat16)
+            for part in range(per_block):
+                heads_out[slot_at, block * per_block + part, 0] = out[
+                    part * length : (part + 1) * length
+                ]
+            return carry
+
+        lax.fori_loop(0, blocks, finish, 0)
+
+    for slot_at in range(slots):
+        for other in others():
+            take_mix(slot_at, other).wait_recv()
+        attend(slot_at)
+        for other in others():
+            send_heads(slot_at, other).start()
+        grads_in[lane, slot_at] = heads_out[slot_at, lane]
+
+    load_qkv.wait()
+    for slot_at in range(slots):
+        for other in others():
+            take_heads(slot_at, other).wait_recv()
+    for other in range(lanes):
+        for kind in range(3):
+            for slot_at in range(slots):
+                start = kind * model + other * width
+                grads_flat[slot_at * length : (slot_at + 1) * length, start : start + width] = (
+                    grads_in[other, slot_at, kind]
+                )
+
+    grad_low = dot_nt(grads_flat[...], up[...])
+    grad_low = grad_low.astype(jnp.bfloat16)
+    total[...] = dot_nn(grad_low, down[...])
+
+    def qkv_body(index, carry):
+        columns = at_columns(index, TILE)
+        total[...] += dot_nt(grads_flat[:, columns], qkv_weight[:, columns])
+        return carry
+
+    lax.fori_loop(0, 3 * model // TILE, qkv_body, 0)
+    result[...] = grad_attended[...] + norm_backward(hidden[...], gains[0:1], total[...])
+    ranks = down.shape[0]
+    adapters[0:ranks] = dot_tn(grad_low, normed[...])
+    scale = ADAPTER_ALPHA / (ranks // 2)
+    low_values = (low_rank[...] * scale).astype(jnp.bfloat16)
+    owner = lax.broadcasted_iota(jnp.int32, (ranks, model), 0)
+    up_query = dot_tn(low_values, grads_flat[:, :model])
+    up_value = dot_tn(low_values, grads_flat[:, 2 * model :])
+    adapters[ranks : 2 * ranks] = jnp.where(owner < ranks // 2, up_query, up_value)
+    for slot_at in range(slots):
+        for other in others():
+            send_mix(slot_at, other).wait_send()
+            send_heads(slot_at, other).wait_send()
+
+
+def fast_sum(sizes, terms):
+    count = math.prod(sizes)
+    pieces = terms.reshape(count, -1, 128)
+    vmem = pl.BlockSpec(memory_space=pltpu.VMEM)
+    summed = pl.pallas_call(
+        partial(fast_sum_kernel, sizes),
+        out_shape=jax.ShapeDtypeStruct(pieces.shape, jnp.float32),
+        in_specs=[vmem],
+        out_specs=vmem,
+        scratch_shapes=[pltpu.VMEM(pieces.shape, jnp.float32)]
+        + [pltpu.SemaphoreType.DMA((count,))] * 4,
+        name="adapter_sum",
+        compiler_params=pltpu.CompilerParams(collective_id=0, has_side_effects=True),
+    )(pieces)
+    return summed.reshape(terms.shape)
+
+
+def fast_sum_kernel(sizes, terms, total, landing, send_sem, recv_sem, spread_send, spread_recv):
+    chips, lanes = sizes
+    count = chips * lanes
+    mine = lax.axis_index("dp") * lanes + lax.axis_index("sp")
+
+    def place(step):
+        other = lax.rem(mine + step, count)
+        return other, (other // lanes, lax.rem(other, lanes))
+
+    def scatter(step):
+        other, device = place(step)
+        return remote(
+            terms.at[other], landing.at[step], send_sem.at[step], recv_sem.at[step], device
+        )
+
+    def spread(step):
+        _, device = place(step)
+        return remote(
+            total.at[mine], total.at[mine], spread_send.at[step], spread_recv.at[step], device
+        )
+
+    greet([place(step)[1] for step in range(1, count)])
+    for step in range(1, count):
+        scatter(step).start()
+    landing[0] = terms[mine]
+    for step in range(1, count):
+        scatter(step).wait()
+    total[mine] = jnp.sum(landing[...], axis=0)
+    for step in range(1, count):
+        spread(step).start()
+    for step in range(1, count):
+        spread(step).wait()
+
+
+def forward_call(layer, sizes, hidden, begin, shards, extras):
+    chips, lanes = sizes
+    rows, model = hidden.shape
+    slots, blocks = begin.shape[:2]
+    length = rows // slots
+    width = model // lanes
+    heads = width // HEAD_SIZE
+    hidden_units = shards[2].shape[2]
+    vmem = pl.BlockSpec(memory_space=pltpu.VMEM)
+    anywhere = pl.BlockSpec(memory_space=pl.ANY)
+    low, full = jnp.bfloat16, jnp.float32
+    shape = jax.ShapeDtypeStruct
+    dma = pltpu.SemaphoreType.DMA
+    return pl.pallas_call(
+        partial(forward_kernel, layer, sizes),
+        out_shape=(
+            shape((rows, model), full),
+            shape((rows, model), low),
+            shape((rows, extras[-2].shape[0]), full),
+            shape((lanes, 3, slots, length, width), low),
+            shape((slots, lanes, length, width), low),
+            shape((slots, blocks, 1, heads * BLOCK), full),
+            shape((rows, model), full),
+            shape((rows, hidden_units), low),
+        )
+        + tuple(shape((chips * shard.shape[1], shard.shape[2]), low) for shard in shards),
+        in_specs=[vmem] * 2 + [anywhere] * 4 + [vmem] * len(extras),
+        out_specs=(vmem,) * 8 + (anywhere,) * 4,
+        scratch_shapes=[
+            pltpu.VMEM((2, model, TILE), low),
+            pltpu.VMEM((2, TILE, model), low),
+            pltpu.VMEM((model, model), low),
+            pltpu.VMEM((slots, lanes, 3, length, width), low),
+            pltpu.VMEM((lanes, slots, length, width), low),
+            pltpu.VMEM((blocks, BLOCK, heads * BLOCK), full),
+            pltpu.VMEM((hidden_units // TILE, rows, TILE), low),
+            pltpu.VMEM((rows, model), full),
+            dma((2, 2)),
+            dma,
+            dma((slots, lanes)),
+            dma((slots, lanes)),
+            dma((slots, lanes)),
+            dma((slots, lanes)),
+            dma((4, 6)),
+            dma((4, 6)),
+            dma((4, 3)),
+            dma((4, 3)),
+            dma((4,)),
+        ],
+        name="layer_forward",
+        compiler_params=pltpu.CompilerParams(
+            collective_id=1 + layer, has_side_effects=True, vmem_limit_bytes=VMEM_LIMIT
+        ),
+    )(hidden, begin, *shards, *extras)
+
+
+def backward_call(layer, sizes, gradient, hidden, begin, extras, kept):
+    chips, lanes = sizes
+    rows, model = hidden.shape
+    slots, blocks = begin.shape[:2]
+    length = rows // slots
+    width = model // lanes
+    heads = width // HEAD_SIZE
+    vmem = pl.BlockSpec(memory_space=pltpu.VMEM)
+    anywhere = pl.BlockSpec(memory_space=pl.ANY)
+    low, full = jnp.bfloat16, jnp.float32
+    shape = jax.ShapeDtypeStruct
+    dma = pltpu.SemaphoreType.DMA
+    ranks = extras[1].shape[0]
+    return pl.pallas_call(
+        partial(backward_kernel, sizes),
+        out_shape=(shape((rows, model), full), shape((2 * ranks, model), full)),
+        in_specs=[vmem] * (3 + len(extras) + 7) + [anywhere] * 4,
+        out_specs=(vmem, vmem),
+        scratch_shapes=[
+            pltpu.VMEM((2, model, TILE), low),
+            pltpu.VMEM((2, TILE, model), low),
+            pltpu.VMEM((model, model), low),
+            pltpu.VMEM((model, 3 * model), low),
+            pltpu.VMEM((rows, model), full),
+            pltpu.VMEM((rows, model), full),
+            pltpu.VMEM((slots, lanes, length, width), low),
+            pltpu.VMEM((lanes, slots, length, width), low),
+            pltpu.VMEM((blocks, heads * BLOCK, width), low),
+            pltpu.VMEM((blocks, heads * BLOCK, width), low),
+            pltpu.VMEM((blocks, 1, heads * BLOCK), full),
+            pltpu.VMEM((blocks, heads * BLOCK, width), full),
+            pltpu.VMEM((BLOCK, width), full),
+            pltpu.VMEM((BLOCK, width), full),
+            pltpu.VMEM((slots, lanes, 3, length, width), low),
+            pltpu.VMEM((lanes, slots, 3, length, width), low),
+            pltpu.VMEM((rows, 3 * model), low),
+            dma((2, 2)),
+            dma((2,)),
+            dma((slots, lanes)),
+            dma((slots, lanes)),
+            dma((slots, lanes)),
+            dma((slots, lanes)),
+        ],
+        name="layer_backward",
+        compiler_params=pltpu.CompilerParams(
+            collective_id=8 + layer, has_side_effects=True, vmem_limit_bytes=VMEM_LIMIT
+        ),
+    )(gradient, hidden, begin, *extras, *kept)
+
+
+def fast_body(
+    sizes,
+    first_layer_input,
+    cotangent,
+    document_begin,
+    query_key_value_weight,
+    attention_out_weight,
+    feedforward_in_weight,
+    feedforward_out_weight,
+    query_value_bias,
+    attention_out_bias,
+    feedforward_in_bias,
+    feedforward_out_bias,
+    layernorm_gain,
+    layernorm_bias,
+    adapter_down_maps,
+    adapter_up_maps,
+):
+    chips, lanes = sizes
+    slots, length, model = first_layer_input.shape
+    layers, _, rank, _ = adapter_down_maps.shape
+    heads = model // lanes // HEAD_SIZE
+    blocks = lanes * length // BLOCK
+    begin = document_begin.reshape(slots, blocks, 1, BLOCK)
+    begin = jnp.concatenate([begin] * heads, -1)
+    shards = (
+        query_key_value_weight,
+        attention_out_weight,
+        feedforward_in_weight,
+        feedforward_out_weight,
+    )
+    adapter_scale = ADAPTER_ALPHA / rank
+    blank = jnp.zeros((rank, model), jnp.bfloat16)
+    plain = jnp.ones((2 * model,), jnp.float32)
+
+    def extras_of(layer):
+        down = adapter_down_maps[layer].reshape(2 * rank, model).astype(jnp.bfloat16)
+        ups = (adapter_scale * adapter_up_maps[layer]).astype(jnp.bfloat16)
+        up = jnp.concatenate(
+            [
+                jnp.concatenate([ups[0], blank, blank], 1),
+                jnp.concatenate([blank, blank, ups[1]], 1),
+            ],
+            0,
+        )
+        bias = query_value_bias[layer]
+        qkv_bias = jnp.stack(
+            [
+                jnp.concatenate([bias[0], jnp.zeros_like(bias[0]), bias[1]]),
+                jnp.concatenate([jnp.full((model,), HEAD_SIZE ** (-0.5), jnp.float32), plain]),
+            ]
+        )
+        return (
+            qkv_bias,
+            attention_out_bias[layer][None],
+            feedforward_in_bias[layer][None],
+            feedforward_out_bias[layer][None],
+            layernorm_gain[layer],
+            layernorm_bias[layer],
+            down,
+            up,
+        )
+
+    hidden = first_layer_input.astype(jnp.float32).reshape(slots * length, model)
+    inputs, kept = [], []
+    for layer in range(layers):
+        inputs.append(hidden)
+        hidden, *state = forward_call(layer, sizes, hidden, begin, shards, extras_of(layer))
+        kept.append(state)
+    gradient = cotangent.astype(jnp.float32).reshape(slots * length, model)
+    terms = [None] * layers
+    for layer in reversed(range(layers)):
+        extras = extras_of(layer)
+        gradient, terms[layer] = backward_call(
+            layer, sizes, gradient, inputs[layer], begin, (extras[4], *extras[6:]), kept[layer]
+        )
+    summed = fast_sum(sizes, jnp.stack(terms))
+    summed = summed * (1.0 / math.sqrt(slots * chips * length * lanes))
+    summed = summed.reshape(layers, 2, 2, rank, model)
+    shape = first_layer_input.shape
+    return hidden.reshape(shape), gradient.reshape(shape), summed[:, 0], summed[:, 1]
+
+
 def solution(mesh):
-    rows, columns = mesh.devices.shape
-    mesh = Mesh(mesh.devices.reshape(rows, columns // 2, 2), ("dp",) + SP)
-    placed = (
-        P("dp", SP, None),
-        P("dp", SP, None),
-        P("dp", None),
-        P(None, "dp", None),
-        P(None, "dp", None),
-        P(None, "dp", None),
-        P(None, "dp", None),
-        P(),
-        P(),
-        P(),
-        P(),
-        P(),
-        P(),
-        P(),
-        P(),
-    )
+    chips, lanes = sizes = tuple(mesh.devices.shape)
+    fast = sizes == (4, 8)
+    token_axes = "sp" if fast else SP
+    if not fast:
+        mesh = Mesh(mesh.devices.reshape(chips, lanes // 2, 2), ("dp",) + SP)
+    tokens = P("dp", token_axes, None)
+    weights = P(None, "dp", None)
     return jax.shard_map(
-        body,
+        partial(fast_body, sizes) if fast else body,
         mesh=mesh,
-        in_specs=placed,
-        out_specs=(P("dp", SP, None), P("dp", SP, None), P(), P()),
+        in_specs=(tokens, tokens, P("dp", None)) + (weights,) * 4 + (P(),) * 8,
+        out_specs=(tokens, tokens, P(), P()),
         check_vma=False,
     )

time: 684 us -> 613 us (0.90)
  Pallas kernels: 16.2 us -> 589 us
  waiting for transfers between devices: 279 us -> 0 us
  matrix products: 152 us -> 0 us
  blocking collectives: 78.8 us -> 0 us
  local copies, waits for them, and re-layouts: 72.3 us -> 10.3 us
  other arithmetic: 37.9 us -> 10.4 us
  starting transfers between devices: 23.2 us -> 0 us
  between operations: 15.9 us -> 0.78 us
    pallas_call x1 -> x5, Pallas kernels: 16.2 us -> 589 us  [the longest x2 416 us: forward_call(): pl.pallas_call(partial(forward_kernel, layer, sizes), out_shape=(shape((r...]
    dot_general x66 -> x0, matrix products: 152 us -> none  [the longest x2 22.5 us: layer_backward(): jnp.einsum('stf,df->std', grad_pre, feedforward_in_weight, preferred_elem...]
    all_gather x8 -> x0, waiting for transfers between devices: 149 us -> none  [fetch(): return lax.all_gather(part, ('dp', 'core'), axis=0, tiled=True)]
    all_to_all x5 -> x0, waiting for transfers between devices: 131 us -> none  [the longest x2 72.8 us: layer_forward(): lax.all_to_all(jnp.stack([query_rows, key_rows, value_rows]), SP, split_a...]
    all_to_all x3 -> x0, blocking collectives: 78.8 us -> none  [the longest x1 40.5 us: layer_backward(): lax.all_to_all(jnp.stack([grad_q_h, grad_k_h, grad_v_h]), SP, split_axis=...]
    all_to_all x5 -> x0, starting transfers between devices: 22.4 us -> none  [the longest x2 9.45 us: layer_forward(): lax.all_to_all(jnp.stack([query_rows, key_rows, value_rows]), SP, split_a...]
    another operation x32 -> x1, local copies, waits for them, and re-layouts: 19 us -> 0.01 us  [the longest x14 7.54 us: layer_forward(): queries_h, keys_h, values_h = lax.all_to_all(jnp.stack([query_rows, key_r...]
    while x40 -> x0, local copies, waits for them, and re-layouts: 13.1 us -> none  [the longest x6 6.84 us: layer_backward(): lax.map(slot_backward, (queries_h, keys_h, values_h, document_begin, log_...]
  transfers between devices with their start and end apart: 13 -> 0, of which waited for: 9 -> 0; matrix products, arithmetic and copies ran while one was open for 17% -> 0% of each run, Pallas kernels for 0% -> 0%
where the time goes in v2:
time: 613 us; the launch traced here: 611 us
  Pallas kernels  589 us (96%)
  other arithmetic  10.4 us (2%)
  local copies, waits for them, and re-layouts  10.3 us (2%)
    pallas_call x2, Pallas kernels, forward_call(): pl.pallas_call(partial(forward_kernel, layer, sizes), out_shape=(shape((r...  416 us
    pallas_call x2, Pallas kernels, backward_call(): pl.pallas_call(partial(backward_kernel, sizes), out_shape=(shape((rows, m...  148 us
    pallas_call x1, Pallas kernels, fast_sum(): pl.pallas_call(partial(fast_sum_kernel, sizes), out_shape=jax.ShapeDtypeS...  25.3 us

profile of v2, /device:TPU:0, one launch (start us, length us, event | category | flops | bytes accessed | tf_op | source)
XLA Modules:
  0.0 610.9 jit_solution(3432031851651893738)
XLA Ops:
  0.6 0.7 reshape.61
  1.4 0.8 fusion.10
  2.2 1.4 fusion.11
  3.6 1.4 pad_maximum_fusion.1
  5.0 0.9 convert.6
  5.8 0.6 convert_element_type.22.down
  7.0 1.4 slice_bitcast_fusion.6
  8.4 1.5 fusion.9
  9.9 0.8 multiply_convert_fusion
  10.7 0.6 fusion.5.up
  11.3 0.6 fusion.4.up
  12.0 2.1 bitcast_convert_fusion.1.hidden
  14.1 2.1 bitcast_convert_fusion.gradient
  16.2 209.7 %layer_forward.2 = (f32[256,1024]{1,0:T(8,128)}, bf16[256,1024]{1,0:T(8,128)(2,1)}, f32[256,8]{1,0:T(8,128)}, bf16[8,3,2,128,128]{4,3,2,1,0:T(8,128)(2,1)}, bf16...) custom-call(f32[256,1024]{1,0:T(8,128)} %bitcast_convert_fusion.1.hi, ...), custom_call_target="tpu_custom_call" | custom-call | tf_op jit(solution)/shard_map/layer_forward/pallas_call | solution.py:1249
  225.9 206.2 %layer_forward.3 = (f32[256,1024]{1,0:T(8,128)}, bf16[256,1024]{1,0:T(8,128)(2,1)}, f32[256,8]{1,0:T(8,128)}, bf16[8,3,2,128,128]{4,3,2,1,0:T(8,128)(2,1)}, bf16...) custom-call(f32[256,1024]{1,0:T(8,128)} %get-tuple-element.32.hidden, ...), custom_call_target="tpu_custom_call" | custom-call | tf_op jit(solution)/shard_map/layer_forward/pallas_call | solution.py:1249
  432.2 70.0 %layer_backward.2 = (f32[256,1024]{1,0:T(8,128)}, f32[16,1024]{1,0:T(8,128)}) custom-call(f32[256,1024]{1,0:T(8,128)} %bitcast_convert_fusion.gradient, f32[256,1024]{1,0:T(8,128)} %get-tuple-element.32.hidden, s32[2,4,1,512]{3,2,1,0:T(1,128)} %copy-done.2, f32[2,1024]{1,0:T(2,128)} %get-tuple-element.91.gains, bf16[8,1024]{1,0:T(8,128)(2,1)} %convert_element_type.22.down, ...), custom_call_target="tpu_custom_call" | custom-call | tf_op jit(solution)/shard_map/layer_backward/pallas_call | solution.py:1305
  502.2 78.2 %layer_backward.3 = (f32[256,1024]{1,0:T(8,128)}, f32[16,1024]{1,0:T(8,128)}) custom-call(f32[256,1024]{1,0:T(8,128)} %get-tuple-element.45.gradient, f32[256,1024]{1,0:T(8,128)} %bitcast_convert_fusion.1.hidden, s32[2,4,1,512]{3,2,1,0:T(1,128)} %copy-done.2, f32[2,1024]{1,0:T(2,128)} %get-tuple-element.90.gains, bf16[8,1024]{1,0:T(8,128)(2,1)} %convert_element_type.20.down, ...), custom_call_target="tpu_custom_call" | custom-call | tf_op jit(solution)/shard_map/layer_backward/pallas_call | solution.py:1305
  580.4 0.9 pad_maximum_fusion
  581.4 0.7 copy.23
  582.1 25.3 %adapter_sum.1 = f32[32,8,128]{2,1,0:T(8,128)} custom-call(f32[32,8,128]{2,1,0:T(8,128)} %bitcast.46), custom_call_target="tpu_custom_call" | custom-call | tf_op jit(solution)/shard_map/adapter_sum/pallas_call | solution.py:1189
  607.3 0.9 broadcast_multiply_fusion
  608.3 0.7 slice_bitcast_fusion
  609.0 1.0 copy.27
  609.9 1.0 copy.28
  (16 shorter events, 0.7 us)
Async XLA Ops:
  1.4 14.8 %copy-start.2 = (s32[2,4,1,512]{3,2,1,0:T(1,128)}, s32[2,4,1,512]{3,2,1,0:T(1,128)S(1)}, u32[]{:S(2)}) copy-start(s32[2,4,1,512]{3,2,1,0:T(1,128)S(1)} %constant_dynamic-update-slice_fusion.begin) | copy-start | bytes 49156
  502.2 78.2 %copy-start.3 = (f32[16,1024]{1,0:T(8,128)S(1)}, f32[16,1024]{1,0:T(8,128)}, u32[]{:S(2)}) copy-start(f32[16,1024]{1,0:T(8,128)} %get-tuple-element.59) | copy-start | bytes 196612
  502.2 106.8 %copy-start = (f32[256,1024]{1,0:T(8,128)S(1)}, f32[256,1024]{1,0:T(8,128)}, u32[]{:S(2)}) copy-start(f32[256,1024]{1,0:T(8,128)} %get-tuple-element.33) | copy-start | bytes 3145732
  580.4 29.5 %copy-start.1 = (f32[256,1024]{1,0:T(8,128)S(1)}, f32[256,1024]{1,0:T(8,128)}, u32[]{:S(2)}) copy-start(f32[256,1024]{1,0:T(8,128)} %get-tuple-element.57) | copy-start | bytes 3145732

commit v3 on v1

--- a/solution.py
+++ b/solution.py
@@ -438,30 +438,1037 @@
     return (hidden_state, gradient, grad_down * token_scale, grad_up * token_scale)
 
 
+MESH = pl.DeviceIdType.MESH
+TILE = 512
+LANES = 128
+DEPTH = 4
+VMEM_LIMIT = 60 * 1024 * 1024
+LOW, FULL = jnp.bfloat16, jnp.float32
+
+
+def dot_nn(left, right):
+    return jnp.dot(left, right, preferred_element_type=FULL)
+
+
+def dot_nt(left, right):
+    return lax.dot_general(left, right, (((1,), (1,)), ((), ())), preferred_element_type=FULL)
+
+
+def dot_tn(left, right):
+    return lax.dot_general(left, right, (((0,), (0,)), ((), ())), preferred_element_type=FULL)
+
+
+def normalize(tensor):
+    centred = tensor - jnp.mean(tensor, -1, keepdims=True)
+    spread = jnp.mean(centred * centred, -1, keepdims=True)
+    scale = lax.rsqrt(spread + EPSILON)
+    return centred * scale, scale
+
+
+def norm_backward(tensor, gains, gradient):
+    unit, scale = normalize(tensor)
+    weighted = gradient * gains
+    first = jnp.mean(weighted, -1, keepdims=True)
+    second = jnp.mean(weighted * unit, -1, keepdims=True)
+    return scale * (weighted - first - unit * second)
+
+
+GELU_INNER = math.sqrt(2.0 / math.pi)
+GELU_CUBE = 0.044715
+
+
+def gelu(value):
+    inner = GELU_INNER * (value + GELU_CUBE * (value * value * value))
+    return 0.5 * value * (1.0 + jnp.tanh(inner))
+
+
+def gelu_slope(value):
+    square = value * value
+    bend = jnp.tanh(GELU_INNER * (value + GELU_CUBE * (square * value)))
+    climb = GELU_INNER * (1.0 + 3.0 * GELU_CUBE * square)
+    return 0.5 * (1.0 + bend) + 0.5 * value * (1.0 - bend * bend) * climb
+
+
+def split_heads(rows):
+    heads = rows.shape[1] // HEAD_SIZE
+    owner = lax.broadcasted_iota(jnp.int32, rows.shape, 1) // HEAD_SIZE
+    return jnp.concatenate(
+        [jnp.where(owner == head, rows, jnp.zeros_like(rows)) for head in range(heads)], 0
+    )
+
+
+def join_heads(stacked, length):
+    heads = stacked.shape[0] // HEAD_SIZE
+    joined = [
+        stacked[head * HEAD_SIZE : (head + 1) * HEAD_SIZE, head * length : (head + 1) * length]
+        for head in range(heads)
+    ]
+    return jnp.concatenate(joined, 0).T
+
+
+def remote(source, target, send_sem, recv_sem, device):
+    return pltpu.make_async_remote_copy(
+        src_ref=source,
+        dst_ref=target,
+        send_sem=send_sem,
+        recv_sem=recv_sem,
+        device_id=device,
+        device_id_type=MESH,
+    )
+
+
+def prime(count, copies):
+    for index in range(min(count, DEPTH)):
+        for copy in copies(index, index):
+            copy.start()
+
+
+def stream(count, copies, body):
+    def step(index, carry):
+        slot = lax.rem(index, DEPTH)
+        for copy in copies(index, slot):
+            copy.wait()
+        body(index, slot)
+
+        @pl.when(index + DEPTH < count)
+        def _():
+            for copy in copies(index + DEPTH, slot):
+                copy.start()
+
+        return carry
+
+    lax.fori_loop(0, count, step, 0)
+
+
+def at_columns(index, size):
+    return pl.ds(pl.multiple_of(index * size, size), size)
+
+
+class Gather:
+    def __init__(self, shard, full, stride, offset, columns, place, sems):
+        self.shard, self.full = shard, full
+        self.stride, self.offset, self.columns = stride, offset, columns
+        self.rows = shard.shape[0]
+        self.unit = self.rows // 16
+        chips, chip, lane = place
+        self.chip, self.core, self.side = chip, lax.rem(lane, 2), lax.rem(lane // 2, 2)
+        self.next_x = chip + 1 - 2 * lax.rem(chip, 2)
+        self.next_y = lax.rem(chip + 2, chips)
+        self.far = chips - 1 - chip
+        self.to_x, self.to_y = (self.next_x, lane), (self.next_y, lane)
+        self.to_z = (chip, lane + 2 - 4 * self.side)
+        self.to_core = (chip, lane + 1 - 2 * self.core)
+        self.send_sem, self.recv_sem = sems
+
+    def whole(self, owner, start, count):
+        first = owner * self.stride + self.offset + start
+        return self.full.at[pl.ds(pl.multiple_of(first, 16), count), self.columns]
+
+    def units(self, owner, first, count, own=False):
+        start = (self.core * 8 + first) * self.unit
+        size = count * self.unit
+        if own:
+            return self.shard.at[pl.ds(pl.multiple_of(start, 16), size), self.columns]
+        return self.whole(owner, start, size)
+
+    def hop(self, index):
+        side = self.side
+        owner, first, count, device = (
+            (self.chip, 4 * side, 4, self.to_x),
+            (self.chip, 4 * side, 4, self.to_y),
+            (self.chip, 4 - 4 * side, 4, self.to_x),
+            (self.chip, 4 - 4 * side, 4, self.to_y),
+            (self.next_x, 4 * side, 2, self.to_y),
+            (self.next_y, 4 * side + 2, 2, self.to_x),
+            (self.far, 4 * side, 4, self.to_z),
+            (self.next_x, 0, 8, self.to_core),
+            (self.next_y, 0, 8, self.to_core),
+            (self.far, 0, 8, self.to_core),
+        )[index]
+        return remote(
+            self.units(owner, first, count, own=index < 4),
+            self.units(owner, first, count),
+            self.send_sem.at[index],
+            self.recv_sem.at[index],
+            device,
+        )
+
+    def own(self):
+        return remote(
+            self.shard.at[:, self.columns],
+            self.whole(self.chip, 0, self.rows),
+            self.send_sem.at[10],
+            self.recv_sem.at[10],
+            self.to_core,
+        )
+
+    def begin(self):
+        for index in range(4):
+            self.hop(index).start()
+        self.own().start()
+
+    def pass_on(self):
+        for arrived, onward in ((0, 4), (1, 5)):
+            self.hop(arrived).wait_recv()
+            self.hop(onward).start()
+
+    def trade(self):
+        self.hop(4).wait_recv()
+        self.hop(5).wait_recv()
+        self.hop(6).start()
+        for arrived, onward in ((2, 7), (3, 8)):
+            self.hop(arrived).wait_recv()
+            self.hop(onward).start()
+
+    def cross(self):
+        self.hop(6).wait_recv()
+        self.hop(9).start()
+
+    def arrive(self):
+        for index in range(7, 10):
+            self.hop(index).wait_recv()
+        self.own().wait_recv()
+
+    def drain(self):
+        for index in range(10):
+            self.hop(index).wait_send()
+        self.own().wait_send()
+
+
+def train_kernel(
+    sizes,
+    tokens_in,
+    cotangent_in,
+    begin,
+    shard_qkv,
+    shard_out,
+    shard_in,
+    shard_back,
+    qv_bias,
+    out_bias,
+    in_bias,
+    back_bias,
+    gains,
+    shifts,
+    down_maps,
+    up_maps,
+    output,
+    input_grad,
+    grad_down,
+    grad_up,
+    full_qkv,
+    full_out,
+    full_in,
+    full_back,
+    hidden,
+    tokens_low,
+    cotangent_low,
+    normed,
+    low_rank,
+    heads_in,
+    mixed,
+    log_total,
+    attended,
+    pre_act,
+    tile_in,
+    tile_back,
+    out_weight,
+    qkv_weight,
+    heads_out,
+    mixture,
+    scores,
+    activation,
+    total,
+    gradient,
+    grad_attended,
+    mix_out,
+    mix_in,
+    queries,
+    mix_heads,
+    delta,
+    query_sum,
+    key_sum,
+    value_sum,
+    grads_in,
+    grads_flat,
+    qkv_bias,
+    up_low,
+    down_low,
+    return_out,
+    result_low,
+    terms,
+    landing,
+    landing_chips,
+    summed,
+    tile_sem,
+    load_sem,
+    heads_send,
+    heads_recv,
+    mix_send,
+    mix_recv,
+    move_send,
+    move_recv,
+    sum_send,
+    sum_recv,
+    gather_send,
+    gather_recv,
+):
+    chips, lanes = sizes
+    chip, lane = lax.axis_index("dp"), lax.axis_index("sp")
+    slots, length, model = tokens_in.shape
+    layers, rows, hidden_units = pre_act.shape
+    ranks = down_low.shape[0]
+    group = lanes // slots
+    half, seat = lane // group, lax.rem(lane, group)
+    parts = model // group // LANES
+    heads = LANES // HEAD_SIZE
+    per_tile = TILE // LANES
+    tiles_each = model // TILE
+    shares = hidden_units // TILE
+
+    def gathers_of(layer):
+        model_half, unit_half = 3 * model // 2, hidden_units // 2
+        back_rows = shard_back.shape[1]
+        back_half = back_rows // 2
+        everything = pl.ds(0, model)
+        plans = (
+            (shard_qkv.at[layer], full_qkv, shard_qkv.shape[1], 0, pl.ds(0, model_half)),
+            (shard_qkv.at[layer], full_qkv, shard_qkv.shape[1], 0, pl.ds(model_half, model_half)),
+            (shard_out.at[layer], full_out, shard_out.shape[1], 0, everything),
+            (shard_in.at[layer], full_in, shard_in.shape[1], 0, pl.ds(0, unit_half)),
+            (shard_in.at[layer], full_in, shard_in.shape[1], 0, pl.ds(unit_half, unit_half)),
+            (shard_back.at[layer, pl.ds(0, back_half)], full_back, back_rows, 0, everything),
+            (
+                shard_back.at[layer, pl.ds(back_half, back_half)],
+                full_back,
+                back_rows,
+                back_half,
+                everything,
+            ),
+        )
+        return [
+            Gather(
+                shard,
+                full.at[layer],
+                stride,
+                offset,
+                columns,
+                (chips, chip, lane),
+                (gather_send.at[layer, index], gather_recv.at[layer, index]),
+            )
+            for index, (shard, full, stride, offset, columns) in enumerate(plans)
+        ]
+
+    gathers = [gathers_of(layer) for layer in range(layers)]
+
+    def mates():
+        return [lax.rem(seat + step, group) for step in range(1, group)]
+
+    def device(mate):
+        return (chip, half * group + mate)
+
+    def lane_of(slot):
+        return slot * group + lane // 2
+
+    def move_in(kind, source, target):
+        def copy(slot):
+            return remote(
+                source.at[slot],
+                target.at[pl.ds(pl.multiple_of(lax.rem(lane, 2) * length, length), length)],
+                move_send.at[kind, slot],
+                move_recv.at[kind, lax.rem(lane, 2)],
+                (chip, lane_of(slot)),
+            )
+
+        for slot in range(slots):
+
+            @pl.when(lane_of(slot) != lane)
+            def _():
+                copy(slot).start()
+
+            @pl.when(lane_of(slot) == lane)
+            def _():
+                start = pl.multiple_of(lax.rem(lane, 2) * length, length)
+                target[pl.ds(start, length)] = source[slot]
+
+    def move_in_wait(kind, source, target, sent):
+        for step in range(2):
+            sender = 2 * seat + step
+            copy = remote(
+                source.at[0],
+                target.at[pl.ds(step * length, length)],
+                move_send.at[kind, step],
+                move_recv.at[kind, step],
+                (chip, lane_of(step)),
+            )
+            if sent:
+
+                @pl.when(lane_of(step) != lane)
+                def _():
+                    copy.wait_send()
+
+            else:
+
+                @pl.when(sender != lane)
+                def _():
+                    copy.wait_recv()
+
+    def move_out(kind, source, target):
+        for step in range(2):
+            owner = 2 * seat + step
+            part = pl.ds(step * length, length)
+
+            @pl.when(owner != lane)
+            def _():
+                remote(
+                    source.at[part],
+                    target.at[half],
+                    move_send.at[kind, step],
+                    move_recv.at[kind, half],
+                    (chip, owner),
+                ).start()
+
+            @pl.when(owner == lane)
+            def _():
+                target[half] = source[part]
+
+    def move_out_wait(kind, source, target, sent):
+        for step in range(2):
+            owner = 2 * seat + step
+            copy = remote(
+                source.at[pl.ds(step * length, length)],
+                target.at[step],
+                move_send.at[kind, step],
+                move_recv.at[kind, step],
+                (chip, owner),
+            )
+            if sent:
+
+                @pl.when(owner != lane)
+                def _():
+                    copy.wait_send()
+
+            else:
+
+                @pl.when(lane_of(step) != lane)
+                def _():
+                    copy.wait_recv()
+
+    def heads_copy(part, mate, target, owner):
+        return remote(
+            heads_out.at[mate, part],
+            target.at[owner, part],
+            heads_send.at[part, mate],
+            heads_recv.at[part, owner],
+            device(mate),
+        )
+
+    def mix_copy(part, mate, source, target, owner):
+        return remote(
+            source.at[part, mate],
+            target.at[owner, part],
+            mix_send.at[part, mate],
+            mix_recv.at[part, owner],
+            device(mate),
+        )
+
+    def allowed_pairs(key_block, query_block, diagonal):
+        place = lax.broadcasted_iota(jnp.int32, (rows, heads * rows), 0)
+        begin_row = begin[pl.ds(half, 1), at_columns(query_block, rows)]
+        begin_row = jnp.concatenate([begin_row] * heads, 1) - key_block * rows
+        allowed = place >= begin_row
+        if diagonal:
+            column = lax.broadcasted_iota(jnp.int32, (1, heads * rows), 1)
+            allowed = allowed & (place <= lax.rem(column, rows))
+        return allowed
+
+    def load_params(layer):
+        scale = ADAPTER_ALPHA / (ranks // 2)
+        down = jnp.concatenate([down_maps[layer, 0], down_maps[layer, 1]], 0)
+        down_low[...] = down.astype(LOW)
+        blank = jnp.zeros((ranks // 2, model), FULL)
+        up_query = jnp.concatenate([scale * up_maps[layer, 0], blank], 0)
+        up_value = jnp.concatenate([blank, scale * up_maps[layer, 1]], 0)
+        up_low[:, :model] = up_query.astype(LOW)
+        up_low[:, model : 2 * model] = jnp.zeros((ranks, model), LOW)
+        up_low[:, 2 * model :] = up_value.astype(LOW)
+
+    def forward(layer, following):
+        get_qkv_a, get_qkv_b, get_out, get_in_a, get_in_b, get_back_a, get_back_b = gathers[layer]
+        if layer == 0:
+            get_qkv_a.begin()
+            move_in(0, tokens_in, tokens_low)
+            get_qkv_a.pass_on()
+            get_qkv_b.begin()
+        load_params(layer)
+        qkv_bias[0:1, :model] = qv_bias[layer, 0:1]
+        qkv_bias[0:1, model : 2 * model] = jnp.zeros((1, model), FULL)
+        qkv_bias[0:1, 2 * model :] = qv_bias[layer, 1:2]
+        qkv_bias[1:2, :model] = jnp.full((1, model), HEAD_SIZE ** (-0.5), FULL)
+        qkv_bias[1:2, model:] = jnp.ones((1, 2 * model), FULL)
+        if layer == 0:
+            get_qkv_a.trade()
+            move_in_wait(0, tokens_in, tokens_low, False)
+            hidden[0] = tokens_low[...].astype(FULL)
+        unit, _ = normalize(hidden[layer])
+        normed[layer] = (unit * gains[layer, 0:1] + shifts[layer, 0:1]).astype(LOW)
+        low_rank[layer] = dot_nt(normed[layer], down_low[...])
+        if layer > 0:
+            for part in range(parts):
+                for mate in mates():
+                    heads_copy(part, mate, heads_in.at[layer - 1], seat).wait_send()
+        get_qkv_b.pass_on()
+        get_out.begin()
+        get_in_a.begin()
+        get_qkv_a.cross()
+
+        def qkv_run(first_tile, count):
+            def copies(index, slot):
+                columns = at_columns(first_tile + index, TILE)
+                return [
+                    pltpu.make_async_copy(
+                        full_qkv.at[layer, :, columns], tile_in.at[slot], tile_sem.at[0, slot]
+                    )
+                ]
+
+            def body(index, slot):
+                tile = first_tile + index
+                columns = at_columns(tile, TILE)
+                value = dot_nn(normed[layer], tile_in[slot])
+                value += dot_nn(low_rank[layer].astype(LOW), up_low[:, columns])
+                value += qkv_bias[0:1, columns]
+                value = (value * qkv_bias[1:2, columns]).astype(LOW)
+                kind = tile // tiles_each
+                first = lax.rem(tile, tiles_each) * (per_tile // parts)
+                for step in range(per_tile):
+                    heads_out[first + step // parts, step % parts, kind] = value[
+                        :, step * LANES : (step + 1) * LANES
+                    ]
+
+            prime(count, copies)
+            stream(count, copies, body)
+
+        tile_count = 3 * tiles_each
+        get_qkv_a.arrive()
+        qkv_run(0, tile_count // 2)
+        get_qkv_b.trade()
+        get_qkv_b.cross()
+        get_qkv_b.arrive()
+        qkv_run(tile_count // 2, tile_count // 2)
+        arrivals = heads_in.at[layer]
+        for part in range(parts):
+            for mate in mates():
+                heads_copy(part, mate, arrivals, seat).start()
+            heads_in[layer, seat, part] = heads_out[seat, part]
+        get_out.pass_on()
+        get_in_a.pass_on()
+        get_in_b.begin()
+
+        def attend(part):
+            def query_step(query_block, carry):
+                query_heads = split_heads(heads_in[layer, query_block, part, 0])
+
+                def score_step(key_block, best, diagonal=False):
+                    found = dot_nt(heads_in[layer, key_block, part, 1], query_heads)
+                    allowed = allowed_pairs(key_block, query_block, diagonal)
+                    found = jnp.where(allowed, found, MASKED)
+                    scores[key_block] = found
+                    return jnp.maximum(best, jnp.max(found, 0, keepdims=True))
+
+                lowest = jnp.full((1, heads * rows), MASKED, FULL)
+                best = lax.fori_loop(0, query_block, score_step, lowest)
+                best = score_step(query_block, best, True)
+
+                def mix_step(key_block, carried):
+                    sums, mix = carried
+                    raised = jnp.exp(scores[key_block] - best)
+                    sums = sums + jnp.sum(raised, 0, keepdims=True)
+                    return sums, mix + dot_tn(heads_in[layer, key_block, part, 2], raised.astype(LOW))
+
+                nothing = jnp.zeros((1, heads * rows), FULL), jnp.zeros((LANES, heads * rows), FULL)
+                sums, mix = lax.fori_loop(0, query_block + 1, mix_step, nothing)
+                log_total[layer, part, query_block] = best + jnp.log(sums)
+                mixed[layer, part, query_block] = join_heads(mix * (1.0 / sums), rows).astype(LOW)
+
+                @pl.when(query_block != seat)
+                def _():
+                    mix_copy(part, query_block, mixed.at[layer], mixture, seat).start()
+
+                return carry
+
+            lax.fori_loop(0, group, query_step, 0)
+            mixture[seat, part] = mixed[layer, part, seat]
+
+        load = pltpu.make_async_copy(full_out.at[layer], out_weight, load_sem.at[0])
+        for part in range(parts):
+            for mate in mates():
+                heads_copy(part, mate, arrivals, mate).wait_recv()
+            attend(part)
+            if part == 0:
+                get_out.trade()
+                get_in_b.pass_on()
+                get_back_a.begin()
+                get_in_a.trade()
+        get_back_a.pass_on()
+        get_back_b.begin()
+        get_out.cross()
+        get_out.arrive()
+        load.start()
+        get_in_b.trade()
+        get_in_a.cross()
+
+        for part in range(parts):
+            for mate in mates():
+                mix_copy(part, mate, mixed.at[layer], mixture, mate).wait_recv()
+        load.wait()
+        total[...] = hidden[layer] + out_bias[layer : layer + 1]
+
+        def out_body(index, carry):
+            joined = jnp.concatenate([mixture[index, part] for part in range(parts)], 1)
+            start = pl.multiple_of(index * parts * LANES, parts * LANES)
+            total[...] += dot_nn(joined, out_weight[pl.ds(start, parts * LANES)])
+            return carry
+
+        lax.fori_loop(0, group, out_body, 0)
+        attended[layer] = total[...]
+        unit, _ = normalize(total[...])
+        second = (unit * gains[layer, 1:2] + shifts[layer, 1:2]).astype(LOW)
+
+        def in_run(first_tile, count):
+            def copies(index, slot):
+                columns = at_columns(first_tile + index, TILE)
+                return [
+                    pltpu.make_async_copy(
+                        full_in.at[layer, :, columns], tile_in.at[slot], tile_sem.at[0, slot]
+                    )
+                ]
+
+            def body(index, slot):
+                tile = first_tile + index
+                columns = at_columns(tile, TILE)
+                value = dot_nn(second, tile_in[slot]) + in_bias[layer : layer + 1, columns]
+                pre_act[layer, :, columns] = value.astype(LOW)
+                activation[tile] = gelu(value).astype(LOW)
+
+            prime(count, copies)
+            stream(count, copies, body)
+
+        get_back_a.trade()
+        get_in_a.arrive()
+        in_run(0, shares // 2)
+        get_back_b.pass_on()
+        if following is not None:
+            following[0].begin()
+        get_in_b.cross()
+        get_in_b.arrive()
+        in_run(shares // 2, shares // 2)
+        if following is not None:
+            move_in(1, cotangent_in, cotangent_low)
+        get_back_a.cross()
+        for part in range(parts):
+            for mate in mates():
+                mix_copy(part, mate, mixed.at[layer], mixture, seat).wait_send()
+
+    def back_run(layer, first_tile, ready=False):
+        def copies(index, slot):
+            return [
+                pltpu.make_async_copy(
+                    full_back.at[layer, at_columns(2 * index + first_tile, TILE)],
+                    tile_back.at[slot],
+                    tile_sem.at[1, slot],
+                )
+            ]
+
+        def body(index, slot):
+            total[...] += dot_nn(activation[2 * index + first_tile], tile_back[slot])
+
+        prime(shares // 2, copies)
+        stream(shares // 2, copies, body)
+
+    def grad_tile(index):
+        pairs = shares // 2
+        return 2 * lax.rem(index, pairs) + index // pairs
+
+    def grad_copies(layer, first):
+        def copies(index, slot):
+            columns = at_columns(grad_tile(first + index), TILE)
+            return [
+                pltpu.make_async_copy(
+                    full_in.at[layer, :, columns], tile_in.at[slot], tile_sem.at[0, slot]
+                ),
+                pltpu.make_async_copy(
+                    full_back.at[layer, columns], tile_back.at[slot], tile_sem.at[1, slot]
+                ),
+            ]
+
+        return copies
+
+    def grad_run(layer, low_gradient, first, count):
+        def body(index, slot):
+            columns = at_columns(grad_tile(first + index), TILE)
+            grad_act = dot_nt(low_gradient, tile_back[slot])
+            slope = gelu_slope(pre_act[layer, :, columns].astype(FULL))
+            grad_pre = (slope * grad_act).astype(LOW)
+            total[...] += dot_nt(grad_pre, tile_in[slot])
+
+        stream(count, grad_copies(layer, first), body)
+
+    def backward(layer, last):
+        load_out = pltpu.make_async_copy(full_out.at[layer], out_weight, load_sem.at[0])
+        load_qkv = pltpu.make_async_copy(full_qkv.at[layer], qkv_weight, load_sem.at[1])
+        if last:
+            load_out.start()
+        load_qkv.start()
+        load_params(layer)
+        low_gradient = gradient[...].astype(LOW)
+        total[...] = jnp.zeros_like(total)
+        if last:
+            get_back_a, get_back_b = gathers[layer][5:7]
+            get_back_b.trade()
+            get_back_a.arrive()
+            prime(shares // 2, grad_copies(layer, 0))
+            grad_run(layer, low_gradient, 0, shares // 2)
+            get_back_b.cross()
+            get_back_b.arrive()
+            prime(shares // 2, grad_copies(layer, shares // 2))
+            grad_run(layer, low_gradient, shares // 2, shares // 2)
+        else:
+            grad_run(layer, low_gradient, 0, shares)
+        grad_attended[...] = gradient[...] + norm_backward(
+            attended[layer], gains[layer, 1:2], total[...]
+        )
+        low_attended = grad_attended[...].astype(LOW)
+        load_out.wait()
+        if not last:
+            for part in range(parts):
+                for mate in mates():
+                    mix_copy(part, mate, mix_out, mix_in, seat).wait_send()
+
+        def mix_body(index, carry):
+            start = pl.multiple_of(index * parts * LANES, parts * LANES)
+            value = dot_nt(low_attended, out_weight[pl.ds(start, parts * LANES)]).astype(LOW)
+            for part in range(parts):
+                mix_out[part, index] = value[:, part * LANES : (part + 1) * LANES]
+            return carry
+
+        lax.fori_loop(0, group, mix_body, 0)
+        for part in range(parts):
+            for mate in mates():
+                mix_copy(part, mate, mix_out, mix_in, seat).start()
+            mix_in[seat, part] = mix_out[part, seat]
+            for mate in mates():
+                heads_copy(part, mate, grads_in, seat).wait_send()
+        if last:
+            total[...] = attended[layer] + back_bias[layer : layer + 1]
+            back_run(layer, 0)
+            back_run(layer, 1)
+            result_low[...] = total[...].astype(LOW)
+        if layer > 0:
+            pltpu.make_async_copy(full_out.at[layer - 1], out_weight, load_sem.at[0]).start()
+            prime(shares, grad_copies(layer - 1, 0))
+
+        def attend(part):
+            def prepare(block, carry):
+                queries[block] = split_heads(heads_in[layer, block, part, 0])
+                grads = split_heads(mix_in[block, part])
+                mix_heads[block] = grads
+                mix = jnp.concatenate([mixed[layer, part, block]] * heads, 0)
+                product = grads.astype(FULL) * mix.astype(FULL)
+                delta[block] = jnp.sum(product.T, 0, keepdims=True)
+                query_sum[block] = jnp.zeros_like(query_sum[block])
+                return carry
+
+            lax.fori_loop(0, group, prepare, 0)
+
+            def key_step(key_block, carry):
+                keys = heads_in[layer, key_block, part, 1]
+                values = heads_in[layer, key_block, part, 2]
+                key_sum[...] = jnp.zeros_like(key_sum)
+                value_sum[...] = jnp.zeros_like(value_sum)
+
+                def query_step(query_block, inner, diagonal=False):
+                    query_heads = queries[query_block]
+                    grad_heads = mix_heads[query_block]
+                    found = dot_nt(keys, query_heads)
+                    raised = jnp.exp(found - log_total[layer, part, query_block])
+                    allowed = allowed_pairs(key_block, query_block, diagonal)
+                    weights = jnp.where(allowed, raised, 0.0)
+                    value_sum[...] += dot_nn(weights.astype(LOW), grad_heads)
+                    grad_weights = dot_nt(values, grad_heads)
+                    grad_scores = weights * (grad_weights - delta[query_block])
+                    grad_scores = grad_scores.astype(LOW)
+                    key_sum[...] += dot_nn(grad_scores, query_heads)
+                    query_sum[query_block] += dot_tn(keys, grad_scores)
+                    return inner
+
+                query_step(key_block, 0, True)
+                lax.fori_loop(key_block + 1, group, query_step, 0)
+                out = join_heads(query_sum[key_block], rows).astype(LOW)
+                heads_out[key_block, part, 0] = out * jnp.asarray(HEAD_SIZE ** (-0.5), LOW)
+                heads_out[key_block, part, 1] = key_sum[...].astype(LOW)
+                heads_out[key_block, part, 2] = value_sum[...].astype(LOW)
+
+                @pl.when(key_block != seat)
+                def _():
+                    heads_copy(part, key_block, grads_in, seat).start()
+
+                return carry
+
+            lax.fori_loop(0, group, key_step, 0)
+            grads_in[seat, part] = heads_out[seat, part]
+
+        for part in range(parts):
+            for mate in mates():
+                mix_copy(part, mate, mix_out, mix_in, mate).wait_recv()
+            attend(part)
+
+        load_qkv.wait()
+        for part in range(parts):
+            for mate in mates():
+                heads_copy(part, mate, grads_in, mate).wait_recv()
+            for owner in range(group):
+                for kind in range(3):
+                    start = kind * model + (owner * parts + part) * LANES
+                    grads_flat[:, start : start + LANES] = grads_in[owner, part, kind]
+
+        grad_low = dot_nt(grads_flat[...], up_low[...]).astype(LOW)
+        scale = ADAPTER_ALPHA / (ranks // 2)
+        low_values = (low_rank[layer] * scale).astype(LOW)
+        rank = ranks // 2
+        down_terms = dot_tn(grad_low, normed[layer])
+        terms[4 * layer] = down_terms[:rank]
+        terms[4 * layer + 1] = down_terms[rank:]
+        terms[4 * layer + 2] = dot_tn(low_values, grads_flat[:, :model])[:rank]
+        terms[4 * layer + 3] = dot_tn(low_values, grads_flat[:, 2 * model :])[rank:]
+        if not last:
+            sum_begin()
+        total[...] = dot_nn(grad_low, down_low[...])
+
+        def qkv_body(index, carry):
+            columns = at_columns(index, TILE)
+            total[...] += dot_nt(grads_flat[:, columns], qkv_weight[:, columns])
+            return carry
+
+        lax.fori_loop(0, 3 * tiles_each, qkv_body, 0)
+        gradient[...] = grad_attended[...] + norm_backward(
+            hidden[layer], gains[layer, 0:1], total[...]
+        )
+
+    def sum_lanes():
+        return [
+            remote(
+                terms.at[lax.rem(lane + step, lanes)],
+                landing.at[lane],
+                sum_send.at[0, step],
+                sum_recv.at[0, step],
+                (chip, lax.rem(lane + step, lanes)),
+            )
+            for step in range(1, lanes)
+        ]
+
+    def sum_spread():
+        return [
+            remote(
+                summed.at[lane],
+                summed.at[lane],
+                sum_send.at[1, step],
+                sum_recv.at[1, step],
+                (chip, lax.rem(lane + step, lanes)),
+            )
+            for step in range(1, lanes)
+        ]
+
+    def sum_chips():
+        return [
+            remote(
+                summed,
+                landing_chips.at[chip],
+                sum_send.at[2, step],
+                sum_recv.at[2, step],
+                (lax.rem(chip + step, chips), lane),
+            )
+            for step in range(1, chips)
+        ]
+
+    def sum_begin():
+        for copy in sum_lanes():
+            copy.start()
+        landing[lane] = terms[lane]
+
+    def sum_lanes_finish():
+        for copy in sum_lanes():
+            copy.wait()
+        summed[lane] = jnp.sum(landing[...], axis=0)
+        for copy in sum_spread():
+            copy.start()
+
+    def sum_finish():
+        for copy in sum_spread():
+            copy.wait()
+        for copy in sum_chips():
+            copy.start()
+        landing_chips[chip] = summed[...]
+        for copy in sum_chips():
+            copy.wait()
+        scale = 1.0 / math.sqrt(slots * chips * length * lanes)
+        for layer in range(layers):
+            for kind in range(2):
+                for grads, entry in ((grad_down, kind), (grad_up, 2 + kind)):
+                    terms_of = landing_chips[:, 4 * layer + entry]
+                    grads[layer, kind] = jnp.sum(terms_of, axis=0) * scale
+
+    barrier = pltpu.get_barrier_semaphore()
+    friends = [(chip, lax.rem(lane + step, lanes)) for step in range(1, lanes)]
+    friends += [(lax.rem(chip + step, chips), lane) for step in range(1, chips)]
+    for friend in friends:
+        pl.semaphore_signal(barrier, inc=1, device_id=friend, device_id_type=MESH)
+    pl.semaphore_wait(barrier, len(friends))
+
+    for layer in range(layers):
+        last = layer + 1 == layers
+        forward(layer, None if last else gathers[layer + 1])
+        if not last:
+            total[...] = attended[layer] + back_bias[layer : layer + 1]
+            get_back_a, get_back_b = gathers[layer][5:7]
+            get_back_a.arrive()
+            back_run(layer, 0)
+            gathers[layer + 1][0].pass_on()
+            gathers[layer + 1][1].begin()
+            get_back_b.trade()
+            get_back_b.cross()
+            get_back_b.arrive()
+            back_run(layer, 1)
+            hidden[layer + 1] = total[...]
+            gathers[layer + 1][0].trade()
+    move_in_wait(1, cotangent_in, cotangent_low, False)
+    gradient[...] = cotangent_low[...].astype(FULL)
+    for layer in reversed(range(layers)):
+        last = layer + 1 == layers
+        backward(layer, last)
+        if last:
+            move_out(2, result_low, output)
+    return_out[...] = gradient[...].astype(LOW)
+    sum_lanes_finish()
+    move_out(3, return_out, input_grad)
+    sum_finish()
+    move_out_wait(2, result_low, output, False)
+    move_out_wait(3, return_out, input_grad, False)
+
+    move_in_wait(0, tokens_in, tokens_low, True)
+    move_in_wait(1, cotangent_in, cotangent_low, True)
+    move_out_wait(2, result_low, output, True)
+    move_out_wait(3, return_out, input_grad, True)
+    for layer_gathers in gathers:
+        for gather in layer_gathers:
+            gather.drain()
+    for part in range(parts):
+        for mate in mates():
+            mix_copy(part, mate, mix_out, mix_in, seat).wait_send()
+            heads_copy(part, mate, grads_in, seat).wait_send()
+
+
+def fast_body(sizes, *arrays):
+    chips, lanes = sizes
+    tokens, _, _, *shards = arrays[:7]
+    slots, length, model = tokens.shape
+    layers, kinds, rank, _ = arrays[-1].shape
+    hidden_units = shards[2].shape[2]
+    group = lanes // slots
+    rows, ranks = slots * length, kinds * rank
+    parts, heads = model // group // LANES, LANES // HEAD_SIZE
+    vmem = pl.BlockSpec(memory_space=pltpu.VMEM)
+    anywhere = pl.BlockSpec(memory_space=pl.ANY)
+    shape, dma = jax.ShapeDtypeStruct, pltpu.SemaphoreType.DMA
+    scratch = [
+        ((layers, rows, model), FULL),
+        ((rows, model), LOW),
+        ((rows, model), LOW),
+        ((layers, rows, model), LOW),
+        ((layers, rows, ranks), FULL),
+        ((layers, group, parts, 3, rows, LANES), LOW),
+        ((layers, parts, group, rows, LANES), LOW),
+        ((layers, parts, group, 1, heads * rows), FULL),
+        ((layers, rows, model), FULL),
+        ((layers, rows, hidden_units), LOW),
+        ((DEPTH, model, TILE), LOW),
+        ((DEPTH, TILE, model), LOW),
+        ((model, model), LOW),
+        ((model, 3 * model), LOW),
+        ((group, parts, 3, rows, LANES), LOW),
+        ((group, parts, rows, LANES), LOW),
+        ((group, rows, heads * rows), FULL),
+        ((hidden_units // TILE, rows, TILE), LOW),
+        ((rows, model), FULL),
+        ((rows, model), FULL),
+        ((rows, model), FULL),
+        ((parts, group, rows, LANES), LOW),
+        ((group, parts, rows, LANES), LOW),
+        ((group, heads * rows, LANES), LOW),
+        ((group, heads * rows, LANES), LOW),
+        ((group, 1, heads * rows), FULL),
+        ((group, LANES, heads * rows), FULL),
+        ((rows, LANES), FULL),
+        ((rows, LANES), FULL),
+        ((group, parts, 3, rows, LANES), LOW),
+        ((rows, 3 * model), LOW),
+        ((2, 3 * model), FULL),
+        ((ranks, 3 * model), LOW),
+        ((ranks, model), LOW),
+        ((rows, model), LOW),
+        ((rows, model), LOW),
+        ((lanes, rank, model), FULL),
+        ((lanes, rank, model), FULL),
+        ((chips, lanes, rank, model), FULL),
+        ((lanes, rank, model), FULL),
+    ]
+    semaphores = [
+        (2, DEPTH),
+        (2,),
+        (parts, group),
+        (parts, group),
+        (parts, group),
+        (parts, group),
+        (4, 2),
+        (4, 2),
+        (3, lanes),
+        (3, lanes),
+        (layers, 7, 11),
+        (layers, 7, 11),
+    ]
+    results = pl.pallas_call(
+        partial(train_kernel, sizes),
+        out_shape=(
+            shape((slots, length, model), LOW),
+            shape((slots, length, model), LOW),
+            shape((layers, kinds, rank, model), FULL),
+            shape((layers, kinds, rank, model), FULL),
+        )
+        + tuple(shape((layers, chips * part.shape[1], part.shape[2]), LOW) for part in shards),
+        in_specs=[vmem] * 3 + [anywhere] * 4 + [vmem] * 8,
+        out_specs=(vmem,) * 4 + (anywhere,) * 4,
+        scratch_shapes=[pltpu.VMEM(*entry) for entry in scratch]
+        + [dma(entry) for entry in semaphores],
+        name="train",
+        compiler_params=pltpu.CompilerParams(
+            collective_id=0, has_side_effects=True, vmem_limit_bytes=VMEM_LIMIT
+        ),
+    )(*arrays)
+    output, input_grad, grad_down, grad_up = results[:4]
+    return output.astype(FULL), input_grad.astype(FULL), grad_down, grad_up
+
+
 def solution(mesh):
-    rows, columns = mesh.devices.shape
-    mesh = Mesh(mesh.devices.reshape(rows, columns // 2, 2), ("dp",) + SP)
-    placed = (
-        P("dp", SP, None),
-        P("dp", SP, None),
-        P("dp", None),
-        P(None, "dp", None),
-        P(None, "dp", None),
-        P(None, "dp", None),
-        P(None, "dp", None),
-        P(),
-        P(),
-        P(),
-        P(),
-        P(),
-        P(),
-        P(),
-        P(),
-    )
+    chips, lanes = sizes = tuple(mesh.devices.shape)
+    fast = sizes == (4, 8)
+    token_axes = "sp" if fast else SP
+    if not fast:
+        mesh = Mesh(mesh.devices.reshape(chips, lanes // 2, 2), ("dp",) + SP)
+    tokens = P("dp", token_axes, None)
+    weights = P(None, "dp", None)
     return jax.shard_map(
-        body,
+        partial(fast_body, sizes) if fast else body,
         mesh=mesh,
-        in_specs=placed,
-        out_specs=(P("dp", SP, None), P("dp", SP, None), P(), P()),
+        in_specs=(tokens, tokens, P("dp", None)) + (weights,) * 4 + (P(),) * 8,
+        out_specs=(tokens, tokens, P(), P()),
         check_vma=False,
     )

time: 684 us -> 303 us (0.44)
  waiting for transfers between devices: 279 us -> 0 us
  Pallas kernels: 16.2 us -> 292 us
  matrix products: 152 us -> 0 us
  blocking collectives: 78.8 us -> 0 us
  local copies, waits for them, and re-layouts: 72.3 us -> 2.95 us
  other arithmetic: 37.9 us -> 4.25 us
  starting transfers between devices: 23.2 us -> 0 us
  between operations: 15.9 us -> 0.65 us
    pallas_call x1, Pallas kernels: 16.2 us -> 292 us  [fast_body(): pl.pallas_call(partial(train_kernel, sizes), out_shape=(shape((slots, len...]
    dot_general x66 -> x0, matrix products: 152 us -> none  [the longest x2 22.5 us: layer_backward(): jnp.einsum('stf,df->std', grad_pre, feedforward_in_weight, preferred_elem...]
    all_gather x8 -> x0, waiting for transfers between devices: 149 us -> none  [fetch(): return lax.all_gather(part, ('dp', 'core'), axis=0, tiled=True)]
    all_to_all x5 -> x0, waiting for transfers between devices: 131 us -> none  [the longest x2 72.8 us: layer_forward(): lax.all_to_all(jnp.stack([query_rows, key_rows, value_rows]), SP, split_a...]
    all_to_all x3 -> x0, blocking collectives: 78.8 us -> none  [the longest x1 40.5 us: layer_backward(): lax.all_to_all(jnp.stack([grad_q_h, grad_k_h, grad_v_h]), SP, split_axis=...]
    all_to_all x5 -> x0, starting transfers between devices: 22.4 us -> none  [the longest x2 9.45 us: layer_forward(): lax.all_to_all(jnp.stack([query_rows, key_rows, value_rows]), SP, split_a...]
    another operation x32 -> x0, local copies, waits for them, and re-layouts: 19 us -> none  [the longest x14 7.54 us: layer_forward(): queries_h, keys_h, values_h = lax.all_to_all(jnp.stack([query_rows, key_r...]
    while x40 -> x0, local copies, waits for them, and re-layouts: 13.1 us -> none  [the longest x6 6.84 us: layer_backward(): lax.map(slot_backward, (queries_h, keys_h, values_h, document_begin, log_...]
  transfers between devices with their start and end apart: 13 -> 0, of which waited for: 9 -> 0; matrix products, arithmetic and copies ran while one was open for 17% -> 0% of each run, Pallas kernels for 0% -> 0%
where the time goes in v3:
time: 303 us; the launch traced here: 300 us
  Pallas kernels  292 us (96%)
  other arithmetic  4.25 us (1%)
    pallas_call x1, Pallas kernels, fast_body(): pl.pallas_call(partial(train_kernel, sizes), out_shape=(shape((slots, len...  292 us

profile of v3, /device:TPU:0, one launch (start us, length us, event | category | flops | bytes accessed | tf_op | source)
XLA Modules:
  0.0 299.8 jit_solution(14261619464542346260)
XLA Ops:
  0.6 291.9 %train.1 = (bf16[2,128,1024]{2,1,0:T(8,128)(2,1)}, bf16[2,128,1024]{2,1,0:T(8,128)(2,1)}, f32[2,2,4,1024]{3,2,1,0:T(4,128)}, f32[2,2,4,1024]{3,2,1,0:T(4,128)}, ...) custom-call(bf16[2,128,1024]{2,1,0:T(8,128)(2,1)} %tokens_in.1, ...), custom_call_target="tpu_custom_call" | custom-call | tf_op jit(solution)/shard_map/train/pallas_call | solution.py:1438
  292.6 2.1 convert_element_type.6
  294.7 2.1 convert_element_type.7
  296.8 1.5 copy.21
  298.3 1.5 copy.22

commit v4 on v3

--- a/solution.py
+++ b/solution.py
@@ -442,6 +442,7 @@
 TILE = 512
 LANES = 128
 DEPTH = 4
+SHARED = ((), ())
 VMEM_LIMIT = 60 * 1024 * 1024
 LOW, FULL = jnp.bfloat16, jnp.float32
 
@@ -477,16 +478,12 @@
 GELU_CUBE = 0.044715
 
 
-def gelu(value):
-    inner = GELU_INNER * (value + GELU_CUBE * (value * value * value))
-    return 0.5 * value * (1.0 + jnp.tanh(inner))
-
-
-def gelu_slope(value):
+def gelu_and_slope(value):
     square = value * value
     bend = jnp.tanh(GELU_INNER * (value + GELU_CUBE * (square * value)))
     climb = GELU_INNER * (1.0 + 3.0 * GELU_CUBE * square)
-    return 0.5 * (1.0 + bend) + 0.5 * value * (1.0 - bend * bend) * climb
+    rise = 0.5 * (1.0 + bend)
+    return value * rise, rise + 0.5 * value * (1.0 - bend * bend) * climb
 
 
 def split_heads(rows):
@@ -545,8 +542,8 @@
 
 
 class Gather:
-    def __init__(self, shard, full, stride, offset, columns, place, sems):
-        self.shard, self.full = shard, full
+    def __init__(self, shard, full, stride, offset, columns, shared, place, sems):
+        self.shard, self.full, self.shared = shard, full, shared
         self.stride, self.offset, self.columns = stride, offset, columns
         self.rows = shard.shape[0]
         self.unit = self.rows // 16
@@ -573,17 +570,20 @@
 
     def hop(self, index):
         side = self.side
+        rest = (4 - 3 * side, 3) if self.shared else (4 - 4 * side, 4)
         owner, first, count, device = (
             (self.chip, 4 * side, 4, self.to_x),
             (self.chip, 4 * side, 4, self.to_y),
-            (self.chip, 4 - 4 * side, 4, self.to_x),
-            (self.chip, 4 - 4 * side, 4, self.to_y),
+            (self.chip, *rest, self.to_x),
+            (self.chip, *rest, self.to_y),
             (self.next_x, 4 * side, 2, self.to_y),
             (self.next_y, 4 * side + 2, 2, self.to_x),
             (self.far, 4 * side, 4, self.to_z),
             (self.next_x, 0, 8, self.to_core),
             (self.next_y, 0, 8, self.to_core),
             (self.far, 0, 8, self.to_core),
+            (self.next_x, 7 * side, 1, self.to_z),
+            (self.next_y, 7 * side, 1, self.to_z),
         )[index]
         return remote(
             self.units(owner, first, count, own=index < 4),
@@ -597,8 +597,8 @@
         return remote(
             self.shard.at[:, self.columns],
             self.whole(self.chip, 0, self.rows),
-            self.send_sem.at[10],
-            self.recv_sem.at[10],
+            self.send_sem.at[12],
+            self.recv_sem.at[12],
             self.to_core,
         )
 
@@ -613,16 +613,18 @@
             self.hop(onward).start()
 
     def trade(self):
+        for arrived, onward in ((2, 10), (3, 11)) if self.shared else ((2, 7), (3, 8)):
+            self.hop(arrived).wait_recv()
+            self.hop(onward).start()
         self.hop(4).wait_recv()
         self.hop(5).wait_recv()
         self.hop(6).start()
-        for arrived, onward in ((2, 7), (3, 8)):
+
+    def cross(self):
+        pairs = ((10, 7), (11, 8)) if self.shared else ()
+        for arrived, onward in pairs + ((6, 9),):
             self.hop(arrived).wait_recv()
             self.hop(onward).start()
-
-    def cross(self):
-        self.hop(6).wait_recv()
-        self.hop(9).start()
 
     def arrive(self):
         for index in range(7, 10):
@@ -630,7 +632,7 @@
         self.own().wait_recv()
 
     def drain(self):
-        for index in range(10):
+        for index in range(12 if self.shared else 10):
             self.hop(index).wait_send()
         self.own().wait_send()
 
@@ -669,7 +671,7 @@
     mixed,
     log_total,
     attended,
-    pre_act,
+    slope,
     tile_in,
     tile_back,
     out_weight,
@@ -716,10 +718,11 @@
     chips, lanes = sizes
     chip, lane = lax.axis_index("dp"), lax.axis_index("sp")
     slots, length, model = tokens_in.shape
-    layers, rows, hidden_units = pre_act.shape
+    layers, rows, hidden_units = slope.shape
     ranks = down_low.shape[0]
     group = lanes // slots
     half, seat = lane // group, lax.rem(lane, group)
+    side = seat // 2
     parts = model // group // LANES
     heads = LANES // HEAD_SIZE
     per_tile = TILE // LANES
@@ -753,6 +756,7 @@
                 stride,
                 offset,
                 columns,
+                index in SHARED[layer],
                 (chips, chip, lane),
                 (gather_send.at[layer, index], gather_recv.at[layer, index]),
             )
@@ -762,7 +766,10 @@
     gathers = [gathers_of(layer) for layer in range(layers)]
 
     def mates():
-        return [lax.rem(seat + step, group) for step in range(1, group)]
+        return [lax.rem(seat + 2, group), group - 1 - seat, seat + 1 - 2 * lax.rem(seat, 2)]
+
+    def block_at(index):
+        return side * index + (1 - side) * (group - 1 - index)
 
     def device(mate):
         return (chip, half * group + mate)
@@ -965,7 +972,8 @@
         get_in_b.begin()
 
         def attend(part):
-            def query_step(query_block, carry):
+            def query_step(index, carry):
+                query_block = block_at(index)
                 query_heads = split_heads(heads_in[layer, query_block, part, 0])
 
                 def score_step(key_block, best, diagonal=False):
@@ -1047,8 +1055,9 @@
                 tile = first_tile + index
                 columns = at_columns(tile, TILE)
                 value = dot_nn(second, tile_in[slot]) + in_bias[layer : layer + 1, columns]
-                pre_act[layer, :, columns] = value.astype(LOW)
-                activation[tile] = gelu(value).astype(LOW)
+                lifted, steepness = gelu_and_slope(value)
+                slope[layer, :, columns] = steepness.astype(LOW)
+                activation[tile] = lifted.astype(LOW)
 
             prime(count, copies)
             stream(count, copies, body)
@@ -1069,21 +1078,23 @@
             for mate in mates():
                 mix_copy(part, mate, mixed.at[layer], mixture, seat).wait_send()
 
-    def back_run(layer, first_tile, ready=False):
+    def back_copies(layer, first):
         def copies(index, slot):
             return [
                 pltpu.make_async_copy(
-                    full_back.at[layer, at_columns(2 * index + first_tile, TILE)],
+                    full_back.at[layer, at_columns(grad_tile(first + index), TILE)],
                     tile_back.at[slot],
                     tile_sem.at[1, slot],
                 )
             ]
 
+        return copies
+
+    def back_run(layer, first, count):
         def body(index, slot):
-            total[...] += dot_nn(activation[2 * index + first_tile], tile_back[slot])
-
-        prime(shares // 2, copies)
-        stream(shares // 2, copies, body)
+            total[...] += dot_nn(activation[grad_tile(first + index)], tile_back[slot])
+
+        stream(count, back_copies(layer, first), body)
 
     def grad_tile(index):
         pairs = shares // 2
@@ -1107,8 +1118,7 @@
         def body(index, slot):
             columns = at_columns(grad_tile(first + index), TILE)
             grad_act = dot_nt(low_gradient, tile_back[slot])
-            slope = gelu_slope(pre_act[layer, :, columns].astype(FULL))
-            grad_pre = (slope * grad_act).astype(LOW)
+            grad_pre = (slope[layer, :, columns].astype(FULL) * grad_act).astype(LOW)
             total[...] += dot_nt(grad_pre, tile_in[slot])
 
         stream(count, grad_copies(layer, first), body)
@@ -1139,19 +1149,18 @@
         )
         low_attended = grad_attended[...].astype(LOW)
         load_out.wait()
-        if not last:
+        if last:
+            prime(shares, back_copies(layer, 0))
+        else:
             for part in range(parts):
                 for mate in mates():
                     mix_copy(part, mate, mix_out, mix_in, seat).wait_send()
 
-        def mix_body(index, carry):
-            start = pl.multiple_of(index * parts * LANES, parts * LANES)
+        for mate in mates() + [seat]:
+            start = pl.multiple_of(mate * parts * LANES, parts * LANES)
             value = dot_nt(low_attended, out_weight[pl.ds(start, parts * LANES)]).astype(LOW)
             for part in range(parts):
-                mix_out[part, index] = value[:, part * LANES : (part + 1) * LANES]
-            return carry
-
-        lax.fori_loop(0, group, mix_body, 0)
+                mix_out[part, mate] = value[:, part * LANES : (part + 1) * LANES]
         for part in range(parts):
             for mate in mates():
                 mix_copy(part, mate, mix_out, mix_in, seat).start()
@@ -1160,8 +1169,7 @@
                 heads_copy(part, mate, grads_in, seat).wait_send()
         if last:
             total[...] = attended[layer] + back_bias[layer : layer + 1]
-            back_run(layer, 0)
-            back_run(layer, 1)
+            back_run(layer, 0, shares)
             result_low[...] = total[...].astype(LOW)
         if layer > 0:
             pltpu.make_async_copy(full_out.at[layer - 1], out_weight, load_sem.at[0]).start()
@@ -1176,80 +1184,92 @@
                 product = grads.astype(FULL) * mix.astype(FULL)
                 delta[block] = jnp.sum(product.T, 0, keepdims=True)
                 query_sum[block] = jnp.zeros_like(query_sum[block])
+                key_sum[block] = jnp.zeros_like(key_sum[block])
+                value_sum[block] = jnp.zeros_like(value_sum[block])
                 return carry
 
             lax.fori_loop(0, group, prepare, 0)
 
-            def key_step(key_block, carry):
+            def pair_step(key_block, query_block, diagonal):
                 keys = heads_in[layer, key_block, part, 1]
                 values = heads_in[layer, key_block, part, 2]
-                key_sum[...] = jnp.zeros_like(key_sum)
-                value_sum[...] = jnp.zeros_like(value_sum)
-
-                def query_step(query_block, inner, diagonal=False):
-                    query_heads = queries[query_block]
-                    grad_heads = mix_heads[query_block]
-                    found = dot_nt(keys, query_heads)
-                    raised = jnp.exp(found - log_total[layer, part, query_block])
-                    allowed = allowed_pairs(key_block, query_block, diagonal)
-                    weights = jnp.where(allowed, raised, 0.0)
-                    value_sum[...] += dot_nn(weights.astype(LOW), grad_heads)
-                    grad_weights = dot_nt(values, grad_heads)
-                    grad_scores = weights * (grad_weights - delta[query_block])
-                    grad_scores = grad_scores.astype(LOW)
-                    key_sum[...] += dot_nn(grad_scores, query_heads)
-                    query_sum[query_block] += dot_tn(keys, grad_scores)
+                query_heads = queries[query_block]
+                grad_heads = mix_heads[query_block]
+                found = dot_nt(keys, query_heads)
+                raised = jnp.exp(found - log_total[layer, part, query_block])
+                allowed = allowed_pairs(key_block, query_block, diagonal)
+                weights = jnp.where(allowed, raised, 0.0)
+                value_sum[key_block] += dot_nn(weights.astype(LOW), grad_heads)
+                grad_weights = dot_nt(values, grad_heads)
+                grad_scores = weights * (grad_weights - delta[query_block])
+                grad_scores = grad_scores.astype(LOW)
+                key_sum[key_block] += dot_nn(grad_scores, query_heads)
+                query_sum[query_block] += dot_tn(keys, grad_scores)
+
+            def block_step(index, carry):
+                block = block_at(index)
+                pair_step(block, block, True)
+
+                def inner_step(step, inner):
+                    key_block = block - (1 - side) * step
+                    pair_step(key_block, block + side * step, False)
                     return inner
 
-                query_step(key_block, 0, True)
-                lax.fori_loop(key_block + 1, group, query_step, 0)
-                out = join_heads(query_sum[key_block], rows).astype(LOW)
-                heads_out[key_block, part, 0] = out * jnp.asarray(HEAD_SIZE ** (-0.5), LOW)
-                heads_out[key_block, part, 1] = key_sum[...].astype(LOW)
-                heads_out[key_block, part, 2] = value_sum[...].astype(LOW)
-
-                @pl.when(key_block != seat)
+                lax.fori_loop(1, group - index, inner_step, 0)
+                out = join_heads(query_sum[block], rows).astype(LOW)
+                heads_out[block, part, 0] = out * jnp.asarray(HEAD_SIZE ** (-0.5), LOW)
+                heads_out[block, part, 1] = key_sum[block].astype(LOW)
+                heads_out[block, part, 2] = value_sum[block].astype(LOW)
+
+                @pl.when(block != seat)
                 def _():
-                    heads_copy(part, key_block, grads_in, seat).start()
+                    heads_copy(part, block, grads_in, seat).start()
 
                 return carry
 
-            lax.fori_loop(0, group, key_step, 0)
+            lax.fori_loop(0, group, block_step, 0)
             grads_in[seat, part] = heads_out[seat, part]
 
         for part in range(parts):
             for mate in mates():
                 mix_copy(part, mate, mix_out, mix_in, mate).wait_recv()
             attend(part)
+        def part_columns(source, part, kind):
+            starts = [kind * model + (owner * parts + part) * LANES for owner in range(group)]
+            return jnp.concatenate([source[:, start : start + LANES] for start in starts], 1)
 
         load_qkv.wait()
+        rank = ranks // 2
+        low_values = (low_rank[layer] * (ADAPTER_ALPHA / rank)).astype(LOW)
+        grad_low = jnp.zeros((rows, ranks), FULL)
+        total[...] = jnp.zeros_like(total)
         for part in range(parts):
             for mate in mates():
                 heads_copy(part, mate, grads_in, mate).wait_recv()
-            for owner in range(group):
-                for kind in range(3):
-                    start = kind * model + (owner * parts + part) * LANES
-                    grads_flat[:, start : start + LANES] = grads_in[owner, part, kind]
-
-        grad_low = dot_nt(grads_flat[...], up_low[...]).astype(LOW)
-        scale = ADAPTER_ALPHA / (ranks // 2)
-        low_values = (low_rank[layer] * scale).astype(LOW)
-        rank = ranks // 2
-        down_terms = dot_tn(grad_low, normed[layer])
-        terms[4 * layer] = down_terms[:rank]
-        terms[4 * layer + 1] = down_terms[rank:]
-        terms[4 * layer + 2] = dot_tn(low_values, grads_flat[:, :model])[:rank]
-        terms[4 * layer + 3] = dot_tn(low_values, grads_flat[:, 2 * model :])[rank:]
-        if not last:
-            sum_begin()
-        total[...] = dot_nn(grad_low, down_low[...])
-
-        def qkv_body(index, carry):
-            columns = at_columns(index, TILE)
-            total[...] += dot_nt(grads_flat[:, columns], qkv_weight[:, columns])
-            return carry
-
-        lax.fori_loop(0, 3 * tiles_each, qkv_body, 0)
+            for kind in range(3):
+                joined = [grads_in[owner, part, kind] for owner in range(group)]
+                grads_flat[kind] = jnp.concatenate(joined, 1)
+            for entry, kind in ((2, 0), (3, 2)):
+                grad_low += dot_nt(grads_flat[kind], part_columns(up_low, part, kind))
+                found = dot_tn(low_values, grads_flat[kind])
+                found = found[:rank] if kind == 0 else found[rank:]
+                for owner in range(group):
+                    start = (owner * parts + part) * LANES
+                    terms[4 * layer + entry, :, start : start + LANES] = found[
+                        :, owner * LANES : (owner + 1) * LANES
+                    ]
+            if part == parts - 1:
+                grad_low = grad_low.astype(LOW)
+                down_terms = dot_tn(grad_low, normed[layer])
+                terms[4 * layer] = down_terms[:rank]
+                terms[4 * layer + 1] = down_terms[rank:]
+                if not last:
+                    sum_begin()
+                total[...] += dot_nn(grad_low, down_low[...])
+            for kind in range(3):
+                total[...] += dot_nt(grads_flat[kind], part_columns(qkv_weight, part, kind))
+        if last:
+            move_out(2, result_low, output)
         gradient[...] = grad_attended[...] + norm_backward(
             hidden[layer], gains[layer, 0:1], total[...]
         )
@@ -1331,13 +1351,15 @@
             total[...] = attended[layer] + back_bias[layer : layer + 1]
             get_back_a, get_back_b = gathers[layer][5:7]
             get_back_a.arrive()
-            back_run(layer, 0)
+            prime(shares // 2, back_copies(layer, 0))
+            back_run(layer, 0, shares // 2)
             gathers[layer + 1][0].pass_on()
             gathers[layer + 1][1].begin()
             get_back_b.trade()
             get_back_b.cross()
             get_back_b.arrive()
-            back_run(layer, 1)
+            prime(shares // 2, back_copies(layer, shares // 2))
+            back_run(layer, shares // 2, shares // 2)
             hidden[layer + 1] = total[...]
             gathers[layer + 1][0].trade()
     move_in_wait(1, cotangent_in, cotangent_low, False)
@@ -1345,8 +1367,6 @@
     for layer in reversed(range(layers)):
         last = layer + 1 == layers
         backward(layer, last)
-        if last:
-            move_out(2, result_low, output)
     return_out[...] = gradient[...].astype(LOW)
     sum_lanes_finish()
     move_out(3, return_out, input_grad)
@@ -1365,6 +1385,11 @@
         for mate in mates():
             mix_copy(part, mate, mix_out, mix_in, seat).wait_send()
             heads_copy(part, mate, grads_in, seat).wait_send()
+
+
+def widen_kernel(*refs):
+    for source, target in zip(refs[:4], refs[4:]):
+        target[...] = source[...].astype(FULL)
 
 
 def fast_body(sizes, *arrays):
@@ -1407,10 +1432,10 @@
         ((group, heads * rows, LANES), LOW),
         ((group, 1, heads * rows), FULL),
         ((group, LANES, heads * rows), FULL),
-        ((rows, LANES), FULL),
-        ((rows, LANES), FULL),
+        ((group, rows, LANES), FULL),
+        ((group, rows, LANES), FULL),
         ((group, parts, 3, rows, LANES), LOW),
-        ((rows, 3 * model), LOW),
+        ((3, rows, group * LANES), LOW),
         ((2, 3 * model), FULL),
         ((ranks, 3 * model), LOW),
         ((ranks, model), LOW),
@@ -1432,8 +1457,8 @@
         (4, 2),
         (3, lanes),
         (3, lanes),
-        (layers, 7, 11),
-        (layers, 7, 11),
+        (layers, 7, 13),
+        (layers, 7, 13),
     ]
     results = pl.pallas_call(
         partial(train_kernel, sizes),
@@ -1453,8 +1478,18 @@
             collective_id=0, has_side_effects=True, vmem_limit_bytes=VMEM_LIMIT
         ),
     )(*arrays)
-    output, input_grad, grad_down, grad_up = results[:4]
-    return output.astype(FULL), input_grad.astype(FULL), grad_down, grad_up
+    return pl.pallas_call(
+        widen_kernel,
+        out_shape=(
+            shape((slots, length, model), FULL),
+            shape((slots, length, model), FULL),
+            shape((layers, kinds, rank, model), FULL),
+            shape((layers, kinds, rank, model), FULL),
+        ),
+        in_specs=[vmem] * 4,
+        out_specs=(vmem,) * 4,
+        name="widen",
+    )(*results[:4])
 
 
 def solution(mesh):

time: 303 us -> 288 us (0.950)
  Pallas kernels: 292 us -> 283 us
  other arithmetic: 4.25 us -> 0 us
    pallas_call x1, Pallas kernels: 292 us -> 281 us  [fast_body(): pl.pallas_call(partial(train_kernel, sizes), out_shape=(shape((slots, len...]
    convert_element_type x2 -> x0, other arithmetic: 4.25 us -> none  [fast_body(): return (output.astype(FULL), input_grad.astype(FULL), grad_down, grad_up)]
where the time goes in v4:
time: 288 us; the launch traced here: 284 us
  Pallas kernels  283 us (98%)
    pallas_call x1, Pallas kernels, fast_body(): pl.pallas_call(partial(train_kernel, sizes), out_shape=(shape((slots, len...  281 us

profile of v4, /device:TPU:0, one launch (start us, length us, event | category | flops | bytes accessed | tf_op | source)
XLA Modules:
  0.0 283.9 jit_solution(14322756498922678068)
XLA Ops:
  0.6 280.6 %train.1 = (bf16[2,128,1024]{2,1,0:T(8,128)(2,1)}, bf16[2,128,1024]{2,1,0:T(8,128)(2,1)}, f32[2,2,4,1024]{3,2,1,0:T(4,128)}, f32[2,2,4,1024]{3,2,1,0:T(4,128)}, ...) custom-call(bf16[2,128,1024]{2,1,0:T(8,128)(2,1)} %tokens_in.1, ...), custom_call_target="tpu_custom_call" | custom-call | tf_op jit(solution)/shard_map/train/pallas_call | solution.py:1463
  281.2 2.6 widen.1

commit v5 on v4

--- a/solution.py
+++ b/solution.py
@@ -1017,13 +1017,13 @@
                 get_in_b.pass_on()
                 get_back_a.begin()
                 get_in_a.trade()
+        get_out.cross()
         get_back_a.pass_on()
         get_back_b.begin()
-        get_out.cross()
+        get_in_b.trade()
+        get_in_a.cross()
         get_out.arrive()
         load.start()
-        get_in_b.trade()
-        get_in_a.cross()
 
         for part in range(parts):
             for mate in mates():

time: 288 us -> 288 us (level)
  no operation moved by 1% of the time
where the time goes in v5:
time: 288 us; the launch traced here: 284 us
  Pallas kernels  283 us (98%)
    pallas_call x1, Pallas kernels, fast_body(): pl.pallas_call(partial(train_kernel, sizes), out_shape=(shape((slots, len...  281 us

profile of v5, /device:TPU:0, one launch (start us, length us, event | category | flops | bytes accessed | tf_op | source)
XLA Modules:
  0.0 283.9 jit_solution(9270880446553954002)
XLA Ops:
  0.6 280.6 %train.1 = (bf16[2,128,1024]{2,1,0:T(8,128)(2,1)}, bf16[2,128,1024]{2,1,0:T(8,128)(2,1)}, f32[2,2,4,1024]{3,2,1,0:T(4,128)}, f32[2,2,4,1024]{3,2,1,0:T(4,128)}, ...) custom-call(bf16[2,128,1024]{2,1,0:T(8,128)(2,1)} %tokens_in.1, ...), custom_call_target="tpu_custom_call" | custom-call | tf_op jit(solution)/shard_map/train/pallas_call | solution.py:1463
  281.2 2.6 widen.1
